TPU v7x, 128 devices: a whole 4x4x4 slice. The times are simulated.
128 devices in a mesh: lev: 8 (over x, core), gy: 16 (over z, y).
Axes of the slice: x: 4, y: 4, z: 4, core: 2. Of those that a mesh axis runs over, the one named last changes fastest.
Arguments:
- forcing: bfloat16 [8, 32, 1536, 1024], P('lev', None, 'gy'), may hold values from -6 to 6
- spectral_weight: bfloat16 [2, 128, 32, 32, 128], P(None, 'gy'), may hold values from -4.1875 to 4.1875
- point_weight: bfloat16 [32, 32], replicated, may hold values from -1 to 1
- point_bias: float32 [32], replicated, may hold values from -3 to 3
- decoder: bfloat16 [4, 32], replicated, may hold values from -1 to 1
- coriolis: float32 [1536], P('gy'), may hold values from -1.5 to 1.5
- layer_depth: float32 [8], replicated, may hold values from 0.5 to 2
Outputs:
- equilibrium: float32 [8, 32, 1536, 1024], P('lev', None, 'gy')
- residual: float32 [3, 8, 1536, 1024], P(None, 'lev', 'gy')
All inputs are finite; a program needn't handle non-finite values.
Results may differ from a plain program's by a relative error of at most 0.015.
Values may be sent and summed in bfloat16 or wider, within the bound.
A program may use at most 128 MiB of HBM per device.

v0:
```python
import math

import jax
import jax.numpy as jnp
from jax import lax
from jax.sharding import PartitionSpec as P

ITERS = 3


def laid_out(pieces, dim):
    lengths = list(pieces.shape[1:])
    lengths[dim] *= pieces.shape[0]
    return jnp.moveaxis(pieces, 0, dim).reshape(lengths)


def copy_for_each(value, axis):
    copies = jnp.broadcast_to(value, (lax.axis_size(axis), *value.shape))
    return lax.all_to_all(copies, axis, split_axis=0, concat_axis=0, tiled=True)


def gather_directly(value, axis, dim):
    return laid_out(copy_for_each(value, axis), dim)


def prefix(value, axis, combine, identity):
    peers, place = (lax.axis_size(axis), lax.axis_index(axis))
    everything = lax.all_gather(value, axis)
    start = jnp.broadcast_to(jnp.asarray(identity, value.dtype), value.shape)

    def hop(k, before):
        reached = k < place
        new = combine(before, everything[k])
        return jnp.where(reached, new, before)

    return lax.fori_loop(0, peers, hop, start)


def from_behind(value, axis, steps):
    count = lax.axis_size(axis)
    initial, last = (max(0, -steps), min(count, count - steps))
    return lax.ppermute(value, axis, [(source, source + steps) for source in range(initial, last)])


def extended(value, sides, width):
    for axis, dim in sides:
        peers, length = (lax.axis_size(axis), value.shape[dim])
        up = [(i, (i + 1) % peers) for i in range(peers)]
        down = [(j, i) for i, j in up]
        last = lax.slice_in_dim(value, length - width, length, axis=dim)
        initial = lax.slice_in_dim(value, 0, width, axis=dim)
        before = lax.ppermute(last, axis, up)
        after = lax.ppermute(initial, axis, down)
        value = jnp.concatenate([before, value, after], axis=dim)
    return value


def angles(row_index, col_index, length):
    phase = row_index[:, None] * col_index[None, :] % length
    return phase.astype(jnp.float32) * (2.0 * math.pi / length)


def signed_modes(length, count):
    index = jnp.arange(count, dtype=jnp.int32)
    return jnp.where(index < count // 2, index, index + (length - count))


def forward_x(length, count):
    turned = angles(jnp.arange(length, dtype=jnp.int32), jnp.arange(count, dtype=jnp.int32), length)
    return jnp.stack([jnp.cos(turned), -jnp.sin(turned)], 0).astype(jnp.bfloat16)


def forward_y(row_index, length, count):
    turned = angles(row_index, signed_modes(length, count), length)
    cosine = jnp.cos(turned)
    sine = jnp.sin(turned)
    return jnp.stack([jnp.stack([cosine, -sine], 1), jnp.stack([sine, cosine], 1)], 0).astype(
        jnp.bfloat16
    )


def inverse_y(row_index, length, count):
    turned = angles(signed_modes(length, count), row_index, length)
    cosine = jnp.cos(turned)
    sine = jnp.sin(turned)
    return jnp.stack([jnp.stack([cosine, sine], 1), jnp.stack([-sine, cosine], 1)], 0).astype(
        jnp.bfloat16
    )


def inverse_x(length, count, total):
    index = jnp.arange(count, dtype=jnp.int32)
    turned = angles(index, jnp.arange(length, dtype=jnp.int32), length)
    factor = jnp.where(index == 0, 1.0, 2.0).astype(jnp.float32)[:, None] / total
    return jnp.stack([factor * jnp.cos(turned), -factor * jnp.sin(turned)], 0).astype(jnp.bfloat16)


def mix_modes(spectrum, weights):
    real_part = spectrum[:, :, 0]
    imag_part = spectrum[:, :, 1]
    weight_real = weights[0].astype(jnp.float32)
    weight_imag = weights[1].astype(jnp.float32)
    out_real = jnp.einsum("klim,kiom->klom", real_part, weight_real) - jnp.einsum(
        "klim,kiom->klom", imag_part, weight_imag
    )
    out_imag = jnp.einsum("klim,kiom->klom", real_part, weight_imag) + jnp.einsum(
        "klim,kiom->klom", imag_part, weight_real
    )
    return jnp.stack([out_real, out_imag], 2).astype(jnp.bfloat16)


def add_terms(earlier, later):
    return earlier + later


def roll_diff(field, axis):
    return (jnp.roll(field, -1, axis) - jnp.roll(field, 1, axis)) * 0.5


def on_device(forcing, spectral_weight, point_weight, point_bias, decoder, coriolis, layer_depth):
    level_count, channels, row_count, cell_count = forcing.shape
    group_size = lax.axis_size("gy")
    group_place = lax.axis_index("gy")
    total_rows = row_count * group_size
    own_mode_count = spectral_weight.shape[1]
    mode_count = own_mode_count * group_size
    ymode_count = spectral_weight.shape[4]
    own_rows = group_place * row_count + jnp.arange(row_count, dtype=jnp.int32)
    every_row = jnp.arange(total_rows, dtype=jnp.int32)
    table_fx = forward_x(cell_count, mode_count)
    table_ix = inverse_x(cell_count, mode_count, cell_count * total_rows)
    source = forcing.astype(jnp.float32) + point_bias[None, :, None, None]
    current = forcing
    updated = source
    for iteration in range(ITERS):
        near_modes = jnp.einsum(
            "lcyx,rxk->lrcky", current, table_fx, preferred_element_type=jnp.float32
        ).astype(jnp.bfloat16)
        all_rows = lax.all_to_all(near_modes, "gy", split_axis=3, concat_axis=4, tiled=True)
        table_fy = forward_y(every_row, total_rows, ymode_count)
        spectrum = jnp.einsum(
            "lrcky,ryqm->klqcm", all_rows, table_fy, preferred_element_type=jnp.float32
        )
        mixed = mix_modes(spectrum, spectral_weight)
        own_iy = inverse_y(own_rows, total_rows, ymode_count)
        own_modes = jnp.einsum(
            "klqcm,qmry->lrcky",
            gather_directly(mixed, "gy", 0),
            own_iy,
            preferred_element_type=jnp.float32,
        ).astype(jnp.bfloat16)
        spread = jnp.einsum(
            "lrcky,rkx->lcyx", own_modes, table_ix, preferred_element_type=jnp.float32
        )
        pointwise = jnp.einsum(
            "lcyx,co->loyx", current, point_weight, preferred_element_type=jnp.float32
        )
        updated = jax.nn.gelu(spread + pointwise + source, approximate=True)
        current = updated.astype(jnp.bfloat16)
    fields = jnp.einsum("lcyx,fc->flyx", updated, decoder.astype(jnp.float32))
    turning = coriolis[:, None]
    east_wind = fields[0]
    north_wind = fields[1]
    upward = fields[2]
    heat = fields[3]
    level_start = lax.axis_index("lev") * level_count
    own_depth = lax.dynamic_slice_in_dim(layer_depth, level_start, level_count, 0)
    inside = jnp.cumsum(own_depth[:, None, None] * heat, axis=0)
    lower_sum = prefix(inside[-1], "lev", add_terms, jnp.zeros_like(inside[-1]))
    geopotential = inside + lower_sum[None]
    lower_wind = from_behind(upward[-1], "lev", 1)
    below_level = jnp.concatenate([lower_wind[None], upward[:-1]], 0)
    rimmed = extended(jnp.stack([north_wind, geopotential], 0), (("gy", 2),), 1)
    along_y = (rimmed[:, :, 2:, :] - rimmed[:, :, :-2, :]) * 0.5
    continuity = roll_diff(east_wind, 2) + along_y[0] + upward - below_level
    balance_x = turning * north_wind - roll_diff(geopotential, 2)
    balance_y = turning * east_wind + along_y[1]
    residual = jnp.stack([continuity, balance_x, balance_y], 0)
    return (updated, residual)


def solution(mesh):
    return jax.shard_map(
        on_device,
        mesh=mesh,
        in_specs=(
            P("lev", None, "gy", None),
            P(None, "gy", None, None, None),
            P(),
            P(),
            P(),
            P("gy"),
            P(),
        ),
        out_specs=(P("lev", None, "gy", None), P(None, "lev", "gy", None)),
        check_vma=False,
    )
```

profile of v0, /device:TPU:2, one launch (start us, length us, event | category | flops | bytes accessed | tf_op | source)
XLA Modules:
  0.0 404.5 jit_solution(6902388938620785287)
XLA Ops:
  9.4 4.6 %fusion.82 = bf16[1,2,32,128,96]{3,4,2,1,0:T(8,128)(2,1)S(1)} fusion(bf16[1,32,96,1024]{3,2,1,0:T(8,128)(2,1)} %param.9, bf16[1,1024,128]{2,1,0:T(8,128)(2,1)S(1)} %get-tuple-element.162, bf16[1,1024,128]{2,1,0:T(8,128)(2,1)S(1)} %get-tuple-element.163), kind=kOutput, calls=%fused_computation.97 | convolution fusion | flops 1612447744 | bytes 8388608 | tf_op jit(solution)/shard_map/lcyx,rxk->lrcky/dot_general | solution.py:136
  16.9 8.0 %all-to-all-start = ((bf16[1,2,32,128,96]{4,2,1,0,3:T(8,128)(2,1)}), bf16[1,2,32,128,96]{4,2,1,0,3:T(8,128)(2,1)S(1)}, u32[]{:S(2)}, u32[]{:S(2)}) async-start(bf16[1,2,32,128,96]{4,2,1,0,3:T(8,128)(2,1)} %copy.110), calls=%async_computation | async-start | bytes 4194304 | tf_op jit(solution)/shard_map/all_to_all | solution.py:139
  24.9 3.4 negate_convert_fusion
  29.4 27.2 %all-to-all-done = bf16[1,2,32,128,96]{4,2,1,0,3:T(8,128)(2,1)S(1)} async-done(((bf16[1,2,32,128,96]{4,2,1,0,3:T(8,128)(2,1)}), bf16[1,2,32,128,96]{4,2,1,0,3:T(8,128)(2,1)S(1)}, u32[]{:S(2)}, u32[]{:S(2)}) %all-to-all-start) | async-done | bytes 1572896 | tf_op jit(solution)/shard_map/all_to_all | solution.py:139
  58.3 3.4 reshape.767
  68.1 3.9 all-to-all-start.1
  72.4 3.0 multiply_convert_fusion
  75.4 16.3 %fusion.35 = f32[32,96,1024]{2,0,1:T(8,128)} fusion(bf16[32,96,1024]{2,1,0:T(8,128)(2,1)} %bitcast.403, bf16[32,32]{1,0:T(8,128)(2,1)S(1)} %copy-done), kind=kOutput, calls=%fused_computation.58 | convolution fusion | flops 201326592 | bytes 18876416 | tf_op jit(solution)/shard_map/lcyx,co->loyx/dot_general | solution.py:155
  91.7 10.6 %all-to-all-done.1 = bf16[16,8,1,2,32,128]{5,1,3,4,2,0:T(8,128)(2,1)S(1)} async-done(((bf16[16,8,1,2,32,128]{5,1,3,4,2,0:T(8,128)(2,1)}), bf16[16,8,1,2,32,128]{5,1,3,4,2,0:T(8,128)(2,1)S(1)}, u32[]{:S(2)}, u32[]{:S(2)}) %all-to-all-start.1) | async-done | bytes 2097184 | tf_op jit(solution)/shard_map/all_to_all | solution.py:19
  102.3 17.5 %fusion.7 = bf16[1,32,96,1024]{3,2,1,0:T(8,128)(2,1)} fusion(f32[32,96,1024]{2,0,1:T(8,128)} %fusion.35, bf16[1,32,96,1024]{3,2,1,0:T(8,128)(2,1)} %param.9, f32[32]{0:T(128)S(1)} %copy-done.10, bf16[16,8,1,2,32,128]{5,1,3,4,2,0:T(8,128)(2,1)S(1)} %all-to-all-done.1, bf16[1,128,1024]{2,1,0:T(8,128)(2,1)} %get-tuple-element.164, ...), kind=kOutput, calls=%fused_computation.11 | convolution fusion | flops 2055405568 | bytes 27885696 | tf_op jit(solution)/shard_map/lrcky,rkx->lcyx/dot_general | solution.py:152
  119.8 5.7 %fusion.79 = bf16[1,2,32,128,96]{3,4,2,1,0:T(8,128)(2,1)} fusion(bf16[1,32,96,1024]{3,2,1,0:T(8,128)(2,1)} %fusion.7, bf16[1,1024,128]{2,1,0:T(8,128)(2,1)S(1)} %get-tuple-element.162, bf16[1,1024,128]{2,1,0:T(8,128)(2,1)S(1)} %get-tuple-element.163), kind=kOutput, calls=%fused_computation.96 | convolution fusion | flops 1612447744 | bytes 8388608 | tf_op jit(solution)/shard_map/lcyx,rxk->lrcky/dot_general | solution.py:136
  125.5 3.4 copy.117
  128.9 31.5 %all_to_all.60 = bf16[1,2,32,128,96]{4,2,1,0,3:T(8,128)(2,1)S(1)} all-to-all(bf16[1,2,32,128,96]{4,2,1,0,3:T(8,128)(2,1)S(1)} %copy.117), channel_id=1, replica_groups=mesh['lev'=8,'gy'=16] {'gy'}, dimensions={3} | all-to-all | bytes 3145728 | tf_op jit(solution)/shard_map/all_to_all | solution.py:139
  162.2 3.4 reshape.784
  172.0 4.2 %all-to-all-start.3 = ((bf16[16,8,1,2,32,128]{5,1,3,4,2,0:T(8,128)(2,1)}), bf16[16,8,1,2,32,128]{5,1,3,4,2,0:T(8,128)(2,1)S(1)}, u32[]{:S(2)}, u32[]{:S(2)}) async-start(bf16[16,8,1,2,32,128]{5,1,3,4,2,0:T(8,128)(2,1)} %broadcast_in_dim.19), calls=%async_computation.3 | async-start | bytes 4194304 | tf_op jit(solution)/shard_map/all_to_all | solution.py:19
  176.2 11.6 %fusion.33 = f32[96,1024,32]{1,2,0:T(8,128)} fusion(bf16[32,96,1024]{2,1,0:T(8,128)(2,1)} %bitcast.405, bf16[32,32]{1,0:T(8,128)(2,1)S(1)} %copy-done), kind=kOutput, calls=%fused_computation.56 | convolution fusion | flops 201326592 | bytes 18876416 | tf_op jit(solution)/shard_map/lcyx,co->loyx/dot_general | solution.py:155
  187.8 18.1 %all-to-all-done.3 = bf16[16,8,1,2,32,128]{5,1,3,4,2,0:T(8,128)(2,1)S(1)} async-done(((bf16[16,8,1,2,32,128]{5,1,3,4,2,0:T(8,128)(2,1)}), bf16[16,8,1,2,32,128]{5,1,3,4,2,0:T(8,128)(2,1)S(1)}, u32[]{:S(2)}, u32[]{:S(2)}) %all-to-all-start.3) | async-done | bytes 2097184 | tf_op jit(solution)/shard_map/all_to_all | solution.py:19
  205.8 17.2 %fusion.15 = bf16[1,32,96,1024]{3,2,1,0:T(8,128)(2,1)} fusion(f32[96,1024,32]{1,2,0:T(8,128)} %fusion.33, bf16[1,32,96,1024]{3,2,1,0:T(8,128)(2,1)} %param.9, f32[32]{0:T(128)S(1)} %copy-done.10, bf16[16,8,1,2,32,128]{5,1,3,4,2,0:T(8,128)(2,1)S(1)} %all-to-all-done.3, bf16[1,128,1024]{2,1,0:T(8,128)(2,1)} %get-tuple-element.164, ...), kind=kOutput, calls=%fused_computation.19 | convolution fusion | flops 2055405568 | bytes 27885696 | tf_op jit(solution)/shard_map/lrcky,rkx->lcyx/dot_general | solution.py:152
  223.1 5.7 %fusion.76 = bf16[1,2,32,128,96]{3,4,2,1,0:T(8,128)(2,1)} fusion(bf16[1,32,96,1024]{3,2,1,0:T(8,128)(2,1)} %fusion.15, bf16[1,1024,128]{2,1,0:T(8,128)(2,1)S(1)} %get-tuple-element.162, bf16[1,1024,128]{2,1,0:T(8,128)(2,1)S(1)} %get-tuple-element.163), kind=kOutput, calls=%fused_computation.95 | convolution fusion | flops 1612447744 | bytes 8388608 | tf_op jit(solution)/shard_map/lcyx,rxk->lrcky/dot_general | solution.py:136
  228.8 3.5 copy.124
  232.4 31.2 %all_to_all.61 = bf16[1,2,32,128,96]{4,2,1,0,3:T(8,128)(2,1)S(1)} all-to-all(bf16[1,2,32,128,96]{4,2,1,0,3:T(8,128)(2,1)S(1)} %copy.124), channel_id=1, replica_groups=mesh['lev'=8,'gy'=16] {'gy'}, dimensions={3} | all-to-all | bytes 3145728 | tf_op jit(solution)/shard_map/all_to_all | solution.py:139
  265.3 3.4 reshape.799
  275.1 3.7 all-to-all-start.5
  279.6 11.4 %fusion.31 = f32[96,1024,32]{1,2,0:T(8,128)} fusion(bf16[32,96,1024]{2,1,0:T(8,128)(2,1)} %bitcast.404, bf16[32,32]{1,0:T(8,128)(2,1)S(1)} %copy-done), kind=kOutput, calls=%fused_computation.54 | convolution fusion | flops 201326592 | bytes 18876416 | tf_op jit(solution)/shard_map/lcyx,co->loyx/dot_general | solution.py:155
  291.0 17.5 %all-to-all-done.5 = bf16[16,8,1,2,32,128]{5,1,3,4,2,0:T(8,128)(2,1)S(1)} async-done(((bf16[16,8,1,2,32,128]{5,1,3,4,2,0:T(8,128)(2,1)}), bf16[16,8,1,2,32,128]{5,1,3,4,2,0:T(8,128)(2,1)S(1)}, u32[]{:S(2)}, u32[]{:S(2)}) %all-to-all-start.5) | async-done | bytes 2097184 | tf_op jit(solution)/shard_map/all_to_all | solution.py:19
  308.5 18.7 %fusion.22 = f32[1,32,96,1024]{3,2,1,0:T(8,128)} fusion(f32[96,1024,32]{1,2,0:T(8,128)} %fusion.31, bf16[1,32,96,1024]{3,2,1,0:T(8,128)(2,1)} %param.9, f32[32]{0:T(128)S(1)} %copy-done.10, bf16[16,8,1,2,32,128]{5,1,3,4,2,0:T(8,128)(2,1)S(1)} %all-to-all-done.5, bf16[1,128,1024]{2,1,0:T(8,128)(2,1)S(1)} %copy-done.5, ...), kind=kOutput, calls=%fused_computation.26 | convolution fusion | flops 2052259840 | bytes 34177152 | tf_op jit(solution)/shard_map/lrcky,rkx->lcyx/dot_general | solution.py:152
  327.1 11.4 %fusion.23 = f32[96,1024,4]{1,2,0:T(4,128)S(1)} fusion(f32[32,96,1024]{2,1,0:T(8,128)} %bitcast.406, bf16[4,32]{1,0:T(4,128)(2,1)S(1)} %copy-done.7), kind=kOutput, calls=%fused_computation.33 | convolution fusion | flops 25165824 | bytes 14156032 | tf_op jit(solution)/shard_map/lcyx,fc->flyx/dot_general | solution.py:160
  341.0 24.0 %all-gather.2.cloned.1.call-done = f32[8,96,1024]{2,1,0:T(8,128)} async-done(((f32[1,96,1024]{2,1,0:T(8,128)}), f32[8,96,1024]{2,1,0:T(8,128)}) %all-gather.2.cloned.1.call-update) | async-done | bytes 3145744 | tf_op jit(solution)/shard_map/all_gather | solution.py:28
  365.0 9.3 %while.14 = (s32[]{:T(128)}, f32[96,1024]{1,0:T(8,128)S(1)}, s32[]{:T(128)}, f32[8,96,1024]{2,1,0:T(8,128)}, s32[]{:T(128)}, /*index=5*/s32[]{:T(128)}) while((s32[]{:T(128)}, f32[96,1024]{1,0:T(8,128)S(1)}, s32[]{:T(128)}, f32[8,96,1024]{2,1,0:T(8,128)}, s32[]{:T(128)}, /*index=5*/s32[]{:T(128)}) %tuple.71), condition=%wide.region_1.2_spmd.clone, body=%wide.region_0.1_spmd.clone.sunk | while | flops 294916 | bytes 1179741 | solution.py:36
  374.4 5.2 %collective-permute-start = (f32[2,1,1,1024]{3,2,1,0:T(1,128)S(1)}, f32[2,1,1,1024]{3,2,1,0:T(1,128)S(1)}, u32[]{:S(2)}, u32[]{:S(2)}) collective-permute-start(f32[2,1,1,1024]{3,2,1,0:T(1,128)S(1)} %get-tuple-element.140), channel_id=1, source_target_pairs={{1,0},{2,1},{3,2},{4,3},{5,4},{6,5},{7,6},{8,7},{9,8},{10,9},{11,1... | collective-permute-start | bytes 24584 | tf_op jit(solution)/shard_map/ppermute | solution.py:53
  381.0 5.6 %collective-permute-done.1 = f32[2,1,1,1024]{3,2,1,0:T(1,128)S(1)} collective-permute-done((f32[2,1,1,1024]{3,2,1,0:T(1,128)S(1)}, f32[2,1,1,1024]{3,2,1,0:T(1,128)S(1)}, u32[]{:S(2)}, u32[]{:S(2)}) %collective-permute-start.1) | collective-permute-done | bytes 8224 | tf_op jit(solution)/shard_map/ppermute | solution.py:52
  389.2 6.9 %collective-permute-done.2 = f32[96,1024]{1,0:T(8,128)S(1)} collective-permute-done((f32[96,1024]{1,0:T(8,128)S(1)}, f32[96,1024]{1,0:T(8,128)S(1)}, u32[]{:S(2)}, u32[]{:S(2)}) %collective-permute-start.2) | collective-permute-done | bytes 393248 | tf_op jit(solution)/shard_map/ppermute | solution.py:42
  (85 shorter events, 48.5 us)
Async XLA Ops:
  7.2 68.2 %copy-start = (bf16[32,32]{1,0:T(8,128)(2,1)S(1)}, bf16[32,32]{1,0:T(8,128)(2,1)}, u32[]{:S(2)}) copy-start(bf16[32,32]{1,0:T(8,128)(2,1)} %param.11) | copy-start | bytes 6148
  16.9 39.7 %all-to-all-start = ((bf16[1,2,32,128,96]{4,2,1,0,3:T(8,128)(2,1)}), bf16[1,2,32,128,96]{4,2,1,0,3:T(8,128)(2,1)S(1)}, u32[]{:S(2)}, u32[]{:S(2)}) async-start(bf16[1,2,32,128,96]{4,2,1,0,3:T(8,128)(2,1)} %copy.110), calls=%async_computation | async-start | bytes 4194304 | tf_op jit(solution)/shard_map/all_to_all | solution.py:139
  61.7 2.9 copy-start.1
  68.1 34.2 %all-to-all-start.1 = ((bf16[16,8,1,2,32,128]{5,1,3,4,2,0:T(8,128)(2,1)}), bf16[16,8,1,2,32,128]{5,1,3,4,2,0:T(8,128)(2,1)S(1)}, u32[]{:S(2)}, u32[]{:S(2)}) async-start(bf16[16,8,1,2,32,128]{5,1,3,4,2,0:T(8,128)(2,1)} %broadcast_in_dim.16), calls=%async_computation.1 | async-start | bytes 4194304 | tf_op jit(solution)/shard_map/all_to_all | solution.py:19
  75.4 26.9 %copy-start.10 = (f32[32]{0:T(128)S(1)}, f32[32]{0:T(128)}, u32[]{:S(2)}) copy-start(f32[32]{0:T(128)} %param.12) | copy-start | bytes 388
  165.5 2.9 copy-start.2
  172.0 33.9 %all-to-all-start.3 = ((bf16[16,8,1,2,32,128]{5,1,3,4,2,0:T(8,128)(2,1)}), bf16[16,8,1,2,32,128]{5,1,3,4,2,0:T(8,128)(2,1)S(1)}, u32[]{:S(2)}, u32[]{:S(2)}) async-start(bf16[16,8,1,2,32,128]{5,1,3,4,2,0:T(8,128)(2,1)} %broadcast_in_dim.19), calls=%async_computation.3 | async-start | bytes 4194304 | tf_op jit(solution)/shard_map/all_to_all | solution.py:19
  268.7 2.9 copy-start.3
  273.0 5.9 %copy-start.9 = (f32[8]{0:T(128)S(1)}, f32[8]{0:T(128)}, u32[]{:S(2)}) copy-start(f32[8]{0:T(128)} %param.15) | copy-start | bytes 100
  275.1 33.4 %all-to-all-start.5 = ((bf16[16,8,1,2,32,128]{5,1,3,4,2,0:T(8,128)(2,1)}), bf16[16,8,1,2,32,128]{5,1,3,4,2,0:T(8,128)(2,1)S(1)}, u32[]{:S(2)}, u32[]{:S(2)}) async-start(bf16[16,8,1,2,32,128]{5,1,3,4,2,0:T(8,128)(2,1)} %broadcast_in_dim.20), calls=%async_computation.5 | async-start | bytes 4194304 | tf_op jit(solution)/shard_map/all_to_all | solution.py:19
  278.9 86.2 %all-gather.2.cloned.1.call-start = ((), (), s32[]{:S(2)}) async-start(), calls=%async_computation.6 | async-start | bytes 3538944 | tf_op jit(solution)/shard_map/all_gather | solution.py:28
  279.6 28.9 %copy-start.5 = (bf16[1,128,1024]{2,1,0:T(8,128)(2,1)S(1)}, bf16[1,128,1024]{2,1,0:T(8,128)(2,1)}, u32[]{:S(2)}) copy-start(bf16[1,128,1024]{2,1,0:T(8,128)(2,1)} %get-tuple-element.164) | copy-start | bytes 786436
  279.6 28.9 %copy-start.6 = (bf16[1,128,1024]{2,1,0:T(8,128)(2,1)S(1)}, bf16[1,128,1024]{2,1,0:T(8,128)(2,1)}, u32[]{:S(2)}) copy-start(bf16[1,128,1024]{2,1,0:T(8,128)(2,1)} %get-tuple-element.165) | copy-start | bytes 786436
  291.0 36.1 %copy-start.7 = (bf16[4,32]{1,0:T(4,128)(2,1)S(1)}, bf16[4,32]{1,0:T(4,128)(2,1)}, u32[]{:S(2)}) copy-start(bf16[4,32]{1,0:T(4,128)(2,1)} %param.13) | copy-start | bytes 772
  341.0 33.3 %copy-start.4 = (f32[1,96,1024]{2,1,0:T(8,128)S(1)}, f32[1,96,1024]{2,1,0:T(8,128)}, u32[]{:S(2)}) copy-start(f32[1,96,1024]{2,1,0:T(8,128)} %get-tuple-element.137) | copy-start | bytes 1179652
  374.3 12.5 %copy-start.8 = (f32[96]{0:T(128)S(1)}, f32[96]{0:T(128)}, u32[]{:S(2)}) copy-start(f32[96]{0:T(128)} %param.14) | copy-start | bytes 1156
  374.4 6.6 %collective-permute-start = (f32[2,1,1,1024]{3,2,1,0:T(1,128)S(1)}, f32[2,1,1,1024]{3,2,1,0:T(1,128)S(1)}, u32[]{:S(2)}, u32[]{:S(2)}) collective-permute-start(f32[2,1,1,1024]{3,2,1,0:T(1,128)S(1)} %get-tuple-element.140), channel_id=1, source_target_pairs={{1,0},{2,1},{3,2},{4,3},{5,4},{6,5},{7,6},{8,7},{9,8},{10,9},{11,1... | collective-permute-start | bytes 24584 | tf_op jit(solution)/shard_map/ppermute | solution.py:53
  379.6 7.0 %collective-permute-start.1 = (f32[2,1,1,1024]{3,2,1,0:T(1,128)S(1)}, f32[2,1,1,1024]{3,2,1,0:T(1,128)S(1)}, u32[]{:S(2)}, u32[]{:S(2)}) collective-permute-start(f32[2,1,1,1024]{3,2,1,0:T(1,128)S(1)} %get-tuple-element.141), channel_id=1, source_target_pairs={{0,1},{1,2},{2,3},{3,4},{4,5},{5,6},{6,7},{7,8},{8,9},{9,10},{10,1... | collective-permute-start | bytes 24584 | tf_op jit(solution)/shard_map/ppermute | solution.py:52
  387.0 9.1 %collective-permute-start.2 = (f32[96,1024]{1,0:T(8,128)S(1)}, f32[96,1024]{1,0:T(8,128)S(1)}, u32[]{:S(2)}, u32[]{:S(2)}) collective-permute-start(f32[96,1024]{1,0:T(8,128)S(1)} %get-tuple-element.135), channel_id=1, source_target_pairs={{0,16},{16,32},{32,48},{48,64},{64,80},{80,96},{96,112},{1,17},{17... | collective-permute-start | bytes 1179656 | tf_op jit(solution)/shard_map/ppermute | solution.py:42
Sparse Core Ops, SparseCore 0:
  341.1 23.8 all-gather.1
where the time goes:
time: 412 us; the launch traced here: 405 us
  matrix products  127 us (31%)
  waiting for transfers between devices  111 us (27%)
  blocking collectives  62.7 us (15%)
  local copies, waits for them, and re-layouts  33.9 us (8%)
  other arithmetic  27.7 us (7%)
  starting transfers between devices  27 us (7%)
  between operations  14.7 us (4%)
    all_to_all x2, blocking collectives, on_device(): lax.all_to_all(near_modes, 'gy', split_axis=3, concat_axis=4, tiled=True)  62.7 us
    dot_general x3, matrix products, on_device(): jnp.einsum('lrcky,rkx->lcyx', own_modes, table_ix, preferred_element_type...  53.4 us
    all_to_all x3, waiting for transfers between devices, copy_for_each(): return lax.all_to_all(copies, axis, split_axis=0, concat_axis=0, tiled=True)  46.1 us
    dot_general x3, matrix products, on_device(): jnp.einsum('lcyx,co->loyx', current, point_weight, preferred_element_type...  39.4 us
    all_to_all x1, waiting for transfers between devices, on_device(): lax.all_to_all(near_modes, 'gy', split_axis=3, concat_axis=4, tiled=True)  27.2 us
    all_gather x1, waiting for transfers between devices, prefix(): everything = lax.all_gather(value, axis)  24 us
    dot_general x3, matrix products, on_device(): jnp.einsum('lcyx,rxk->lrcky', current, table_fx, preferred_element_type=j...  16 us
    all_to_all x3, starting transfers between devices, copy_for_each(): return lax.all_to_all(copies, axis, split_axis=0, concat_axis=0, tiled=True)  11.8 us
  transfers between devices with their start and end apart: 8, of which 8 were waited for; matrix products, arithmetic and copies ran while one was open for 12% of the time, Pallas kernels for 0%

commit v1 on v0

v1 whole, which is shorter than its diff:
```python
import functools
import math

import jax
import jax.numpy as jnp
import numpy as np
from jax import lax
from jax.experimental import pallas as pl
from jax.experimental.pallas import tpu as pltpu
from jax.sharding import PartitionSpec as P

C = 32
NX = 1024
NY = 1536
M = 128
ROWS = 96
ITERS = 3
MESH = pl.DeviceIdType.MESH
BF = jnp.bfloat16
F32 = jnp.float32
YC = 32
TILE = 256


def turns(a, b, length):
    phase = (a[:, None] * b[None, :]) % length
    return phase.astype(np.float32) * np.float32(2.0 * math.pi / length)


def lane_modes(half, order):
    p, r, s, j = np.meshgrid(np.array(order), np.arange(2), np.arange(4), np.arange(8), indexing="ij")
    k = 32 * s + 8 * p + j if half == 0 else 32 * p + 8 * s + j
    return k.reshape(-1), r.reshape(-1)


@functools.lru_cache(None)
def x_tables():
    forward, inverse = [], []
    for half in range(2):
        for order in ((0, 1, 2, 3), (1, 0, 3, 2)):
            k, r = lane_modes(half, order)
            turned = turns(np.arange(NX), k, NX)
            wave = np.where(r == 0, np.cos(turned), -np.sin(turned)).astype(np.float32)
            factor = np.where(k == 0, 1.0, 2.0).astype(np.float32) / np.float32(NX * NY)
            forward.append(wave)
            inverse.append((wave * factor[None, :]).T)
    return np.stack(forward).astype(BF), np.stack(inverse).astype(BF)


@functools.lru_cache(None)
def y_tables():
    m = np.arange(M)
    signed = np.where(m < M // 2, m, m + NY - M)
    rows = np.arange(NY)
    turned = turns(rows, signed, NY)
    both = np.concatenate([np.cos(turned), np.sin(turned)], 1).astype(np.float32).astype(BF)
    blocks = both.reshape(4, 4, ROWS, 2 * M)
    first = blocks.reshape(4, 4 * ROWS, 2 * M)
    second = blocks.transpose(1, 0, 2, 3).reshape(4, 4 * ROWS, 2 * M)
    return np.stack([first, second])


def pointwise_matrix(point_weight):
    wt = point_weight.astype(F32).T.reshape(2, 8, 2, C).transpose(0, 2, 1, 3).reshape(C, C)
    full = wt[:, None, :, None] * jnp.eye(16, dtype=F32)[None, :, None, :]
    return full.reshape(C * 16, C * 16).astype(BF)


def decoder_matrix(decoder):
    d = decoder.astype(F32).reshape(4, 2, 8, 2).transpose(0, 1, 3, 2).reshape(4, C)
    full = d[:, None, :, None] * jnp.eye(16, dtype=F32)[None, :, None, :]
    return full.reshape(4 * 16, C * 16).astype(BF)


def gelu(v):
    inner = v * (math.sqrt(2.0 / math.pi) + (math.sqrt(2.0 / math.pi) * 0.044715) * (v * v))
    return (0.5 * v) * (1.0 + jnp.tanh(inner))


def lane_mask(rows):
    return lax.broadcasted_iota(jnp.int32, (rows, 128), 1) < 64


def forward_chunk(load, fwd_ref, near_ref, yc):
    mask = lane_mask(yc)
    for h in range(2):
        outs = []
        for par in range(2):
            lhs = jnp.concatenate([load(16 * h + 2 * pair + par) for pair in range(8)], 0)
            outs.append(jnp.dot(lhs, fwd_ref[2 * h + par], preferred_element_type=F32))
        even, odd = outs
        for pair in range(8):
            rows = slice(pair * yc, (pair + 1) * yc)
            for v in range(2):
                e = even[rows, 128 * v:128 * v + 128]
                o = odd[rows, 128 * v:128 * v + 128]
                near_ref[h, 2 * v, :, 128 * pair:128 * pair + 128] = jnp.where(mask, e, o).astype(BF)
                near_ref[h, 2 * v + 1, :, 128 * pair:128 * pair + 128] = jnp.where(mask, o, e).astype(BF)


def first_body(forcing_ref, fwd_ref, near_ref):
    forward_chunk(lambda c: forcing_ref[c], fwd_ref, near_ref, YC)


def update_chunk(back_ref, state_ref, forcing_ref, kron_ref, bias_ref, inv_ref, sink, yc):
    mask = lane_mask(yc)
    groups = []
    for h in range(2):
        even, odd = [], []
        for pair in range(8):
            b = [back_ref[h, p, :, 128 * pair:128 * pair + 128] for p in range(4)]
            even.append(jnp.concatenate([jnp.where(mask, b[0], b[1]), jnp.where(mask, b[2], b[3])], 1))
            odd.append(jnp.concatenate([jnp.where(mask, b[1], b[0]), jnp.where(mask, b[3], b[2])], 1))
        groups.append(jnp.concatenate(even, 0))
        groups.append(jnp.concatenate(odd, 0))
    for t in range(NX // TILE):
        cols = slice(t * TILE, (t + 1) * TILE)
        mixed = []
        for s in range(yc // 16):
            st = state_ref[:, 16 * s:16 * s + 16, cols].reshape(C * 16, TILE)
            mixed.append(jnp.dot(kron_ref[...], st, preferred_element_type=F32).reshape(4, 8, 16, TILE))
        for g in range(4):
            h, par = g // 2, g % 2
            spread = jnp.dot(groups[g], inv_ref[g, :, cols], preferred_element_type=F32)
            spread = spread.reshape(8, yc, TILE)
            for pair in range(8):
                c = 16 * h + 2 * pair + par
                pw = jnp.concatenate([m[g, pair] for m in mixed], 0)
                v = spread[pair] + pw + (forcing_ref[c, :, cols].astype(F32) + bias_ref[c])
                sink(g, pair, c, cols, gelu(v))


def middle_body(back_ref, state_ref, forcing_ref, kron_ref, bias_ref, fwd_ref, inv_ref, out_ref, near_ref):
    def sink(g, pair, c, cols, value):
        out_ref[c, :, cols] = value.astype(BF)

    update_chunk(back_ref, state_ref, forcing_ref, kron_ref, bias_ref, inv_ref, sink, YC)
    forward_chunk(lambda c: out_ref[c], fwd_ref, near_ref, YC)


def last_body(back_ref, state_ref, forcing_ref, kron_ref, bias_ref, dec_ref, inv_ref, out_ref, fields_ref, hold):
    def sink(g, pair, c, cols, value):
        out_ref[c, :, cols] = value
        hold[8 * g + pair, :, cols] = value.astype(BF)

    update_chunk(back_ref, state_ref, forcing_ref, kron_ref, bias_ref, inv_ref, sink, YC)
    for s in range(YC // 16):
        rows = hold[:, 16 * s:16 * s + 16, :].reshape(C * 16, NX)
        f = jnp.dot(dec_ref[...], rows, preferred_element_type=F32)
        fields_ref[:, 16 * s:16 * s + 16, :] = f.reshape(4, 16, NX)


def rows_spec(lead, yc):
    n = len(lead)
    return pl.BlockSpec((*lead, yc, NX), lambda i: (0,) * n + (i, 0))


def whole_spec(shape):
    return pl.BlockSpec(shape, lambda i: (0,) * len(shape), pipeline_mode=pl.Buffered(1))


SMEM = pl.BlockSpec(memory_space=pltpu.SMEM)
LIMIT = 56 << 20


def first_local(forcing, fwd):
    return pl.pallas_call(
        first_body, name="first_local", grid=(ROWS // YC,),
        in_specs=[rows_spec((C,), YC), whole_spec(fwd.shape)],
        out_specs=rows_spec((2, 4), YC),
        out_shape=jax.ShapeDtypeStruct((2, 4, ROWS, NX), BF),
        compiler_params=pltpu.CompilerParams(vmem_limit_bytes=LIMIT),
    )(forcing, fwd)


def middle_local(back, state, forcing, kron, bias, fwd, inv):
    return pl.pallas_call(
        middle_body, name="middle_local", grid=(ROWS // YC,),
        in_specs=[rows_spec((2, 4), YC), rows_spec((C,), YC), rows_spec((C,), YC), whole_spec(kron.shape), SMEM,
                  whole_spec(fwd.shape), whole_spec(inv.shape)],
        out_specs=[rows_spec((C,), YC), rows_spec((2, 4), YC)],
        out_shape=[jax.ShapeDtypeStruct((C, ROWS, NX), BF), jax.ShapeDtypeStruct((2, 4, ROWS, NX), BF)],
        compiler_params=pltpu.CompilerParams(vmem_limit_bytes=LIMIT),
    )(back, state, forcing, kron, bias, fwd, inv)


def last_local(back, state, forcing, kron, bias, dec, inv):
    return pl.pallas_call(
        last_body, name="last_local", grid=(ROWS // YC,),
        in_specs=[rows_spec((2, 4), YC), rows_spec((C,), YC), rows_spec((C,), YC), whole_spec(kron.shape), SMEM,
                  whole_spec(dec.shape), whole_spec(inv.shape)],
        out_specs=[rows_spec((C,), YC), rows_spec((4,), YC)],
        out_shape=[jax.ShapeDtypeStruct((C, ROWS, NX), F32), jax.ShapeDtypeStruct((4, ROWS, NX), F32)],
        scratch_shapes=[pltpu.VMEM((C, YC, NX), BF)],
        compiler_params=pltpu.CompilerParams(vmem_limit_bytes=LIMIT),
    )(back, state, forcing, kron, bias, dec, inv)


def mode_body(near_ref, weight_ref, ytab_ref, back_ref, wbuf, tabs, r1, part, s2, r2, sp, mx, r3, s4,
              wsem, ss, rs):
    g = lax.axis_index("gy")
    z, y = g // 4, g % 4
    own = ((y, z), (z, y))

    def first_peer(h, a):
        return {"gy": z * 4 + a} if h == 0 else {"gy": a * 4 + y}

    def second_peer(h, b):
        return {"gy": b * 4 + y} if h == 0 else {"gy": z * 4 + b}

    barrier = pltpu.get_barrier_semaphore()
    for h in range(2):
        for d in range(1, 4):
            pl.semaphore_signal(barrier, 1, device_id=first_peer(h, (own[h][0] + d) % 4), device_id_type=MESH)
    weights = pltpu.make_async_copy(weight_ref, wbuf, wsem.at[0])
    weights.start()
    tables = [pltpu.make_async_copy(ytab_ref.at[h, own[h][1]], tabs.at[h], wsem.at[1 + h]) for h in range(2)]
    for t in tables:
        t.start()
    pl.semaphore_wait(barrier, 6)

    def exchange(step, h, peer, src, dst):
        copies = []
        for d in range(1, 4):
            c = pltpu.make_async_remote_copy(
                src_ref=src(d), dst_ref=dst(d), send_sem=ss.at[step, h, d - 1], recv_sem=rs.at[step, h, d - 1],
                device_id=peer(d), device_id_type=MESH)
            c.start()
            copies.append(c)
        return copies

    def wait(copies):
        for c in copies:
            c.wait()

    one = []
    for h in range(2):
        a = own[h][0]
        one.append(exchange(0, h, lambda d: first_peer(h, (a + d) % 4),
                            lambda d: near_ref.at[h, (a + d) % 4], lambda d: r1.at[h, a]))
        r1[h, a] = near_ref[h, a]
    two = []
    for h in range(2):
        a, b = own[h]
        tables[h].wait()
        wait(one[h])

        @pl.loop(0, 4)
        def _(n):
            cols = pl.ds(pl.multiple_of(n * 256, 256), 256)
            x = r1[h, :, :, cols].reshape(4 * ROWS, 256)
            cs = lax.dot_general(tabs[h], x, (((0,), (0,)), ((), ())), preferred_element_type=F32)
            pt = cs.T.reshape(2, 2, 2, 4, 8, 256)
            for pair in range(2):
                for h2 in range(2):
                    q0, q1 = pt[pair, h2, 0], pt[pair, h2, 1]
                    re = q0[..., :M] + q1[..., M:]
                    im = q1[..., :M] - q0[..., M:]
                    both = jnp.concatenate([re, im], 1)
                    c = 2 * (2 * n + pair) + lax.rem(h2 + a, 2)
                    part[h, :, c] = both
                    s2[h, :, c] = both.astype(BF)

        two.append(exchange(1, h, lambda d: second_peer(h, (b + d) % 4),
                            lambda d: s2.at[h, (b + d) % 4], lambda d: r2.at[h, d - 1]))
    for h in range(2):
        b = own[h][1]
        wait(two[h])

        @pl.loop(0, 16)
        def _(c):
            total = part[h, b, c]
            for d in range(3):
                total = total + r2[h, d, c].astype(F32)
            sp[16 * h + c] = total

    weights.wait()
    for j in range(8):
        def add(i, acc):
            ar, ai = acc
            wr = wbuf[0, j, i].astype(F32)
            wi = wbuf[1, j, i].astype(F32)
            sr = jnp.broadcast_to(sp[i, pl.ds(j, 1), :], (C, M))
            si = jnp.broadcast_to(sp[i, pl.ds(8 + j, 1), :], (C, M))
            return ar + (sr * wr - si * wi), ai + (sr * wi + si * wr)

        zero = jnp.zeros((C, M), F32)
        ar, ai = lax.fori_loop(0, C, add, (zero, zero), unroll=4)
        mx[pl.ds(j, C, stride=16), :] = ar
        mx[pl.ds(8 + j, C, stride=16), :] = ai
    three = []
    for h in range(2):
        b = own[h][1]
        r3[h, b] = mx[256 * h:256 * h + 256, :].reshape(16, 16, M).astype(BF)
        three.append(exchange(2, h, lambda d: second_peer(h, (b + d) % 4),
                              lambda d: r3.at[h, b], lambda d: r3.at[h, b]))
    four = []
    for h in range(2):
        a = own[h][0]
        wait(three[h])

        @pl.loop(0, 4)
        def _(n):
            rows = []
            for pair in range(2):
                for h2 in range(2):
                    c = 2 * (2 * n + pair) + lax.rem(h2 + a, 2)
                    block = r3[h, :, c].astype(F32).reshape(4, 2, 8, M)
                    re = block[:, 0].reshape(32, M)
                    im = block[:, 1].reshape(32, M)
                    rows.append(jnp.concatenate([re, -im], 1))
                    rows.append(jnp.concatenate([im, re], 1))
            m2 = jnp.concatenate(rows, 0).astype(BF)
            out = lax.dot_general(tabs[h], m2, (((1,), (1,)), ((), ())), preferred_element_type=F32)
            s4[h, :, :, pl.ds(pl.multiple_of(n * 256, 256), 256)] = out.reshape(4, ROWS, 256).astype(BF)

        four.append(exchange(3, h, lambda d: first_peer(h, (a + d) % 4),
                             lambda d: s4.at[h, (a + d) % 4], lambda d: back_ref.at[h, a]))
        back_ref[h, a] = s4[h, a]
    for h in range(2):
        wait(four[h])


def mode_step(near, weights, ytab):
    shape = (2, 4, ROWS, NX)
    return pl.pallas_call(
        mode_body, name="mode_step",
        in_specs=[pl.BlockSpec(memory_space=pltpu.VMEM), pl.BlockSpec(memory_space=pl.ANY),
                  pl.BlockSpec(memory_space=pl.ANY)],
        out_specs=pl.BlockSpec(memory_space=pltpu.VMEM),
        out_shape=jax.ShapeDtypeStruct(shape, BF),
        scratch_shapes=[
            pltpu.VMEM((2, 8, C, C, M), BF),
            pltpu.VMEM((2, 4 * ROWS, 2 * M), BF),
            pltpu.VMEM(shape, BF),
            pltpu.VMEM((2, 4, 16, 16, M), F32),
            pltpu.VMEM((2, 4, 16, 16, M), BF),
            pltpu.VMEM((2, 3, 16, 16, M), BF),
            pltpu.VMEM((C, 16, M), F32),
            pltpu.VMEM((C * 16, M), F32),
            pltpu.VMEM((2, 4, 16, 16, M), BF),
            pltpu.VMEM(shape, BF),
            pltpu.SemaphoreType.DMA((3,)),
            pltpu.SemaphoreType.DMA((4, 2, 3)),
            pltpu.SemaphoreType.DMA((4, 2, 3)),
        ],
        compiler_params=pltpu.CompilerParams(collective_id=1, has_side_effects=True, vmem_limit_bytes=40 << 20),
    )(near, weights, ytab)


def kron_body(row_ref, wt_ref, col_ref, mask_ref, out_ref):
    left = jnp.dot(row_ref[...], wt_ref[...], preferred_element_type=F32).astype(BF)
    full = jnp.dot(left, col_ref[...], preferred_element_type=F32)
    out_ref[...] = (full * mask_ref[...].astype(F32)).astype(BF)


@functools.lru_cache(None)
def kron_parts():
    order = np.arange(C).reshape(2, 8, 2).transpose(0, 2, 1).reshape(C)
    pick = np.zeros((C, C), np.float32)
    pick[np.arange(C), order] = 1.0
    spread = np.repeat(np.eye(C, dtype=np.float32), 16, 1)
    mask = np.tile(np.eye(16, dtype=np.float32), (C, C))
    four = np.repeat(np.eye(4, dtype=np.float32), 16, 0)
    return [v.astype(BF) for v in (np.repeat(pick, 16, 0), spread, mask, four, pick.T @ spread, mask[:64])]


def kron_matrices(point_weight, decoder):
    rows, cols, mask, dec_rows, dec_cols, dec_mask = [jnp.asarray(v) for v in kron_parts()]

    def call(name, a, w, b, m):
        return pl.pallas_call(kron_body, name=name, out_shape=jax.ShapeDtypeStruct(m.shape, BF))(a, w, b, m)

    return call("pointwise_matrix", rows, point_weight.T, cols, mask), call("decoder_matrix", dec_rows, decoder, dec_cols, dec_mask)


def prefix(value, axis):
    peers, place = lax.axis_size(axis), lax.axis_index(axis)
    everything = lax.all_gather(value, axis)
    kept = jnp.where((jnp.arange(peers) < place)[:, None, None], everything, 0.0)
    return jnp.sum(kept, 0)


def roll_diff(field, axis):
    return (jnp.roll(field, -1, axis) - jnp.roll(field, 1, axis)) * 0.5


def residuals(fields, coriolis, layer_depth):
    turning = coriolis[:, None]
    east_wind, north_wind, upward, heat = fields
    own_depth = lax.dynamic_slice_in_dim(layer_depth, lax.axis_index("lev"), 1, 0)
    inside = own_depth[:, None] * heat
    geopotential = inside + prefix(inside, "lev")
    count = lax.axis_size("lev")
    below = lax.ppermute(upward, "lev", [(i, i + 1) for i in range(count - 1)])
    peers = lax.axis_size("gy")
    up = [(i, (i + 1) % peers) for i in range(peers)]
    down = [(j, i) for i, j in up]
    both = jnp.stack([north_wind, geopotential], 0)
    before = lax.ppermute(both[:, -1:], "gy", up)
    after = lax.ppermute(both[:, :1], "gy", down)
    rimmed = jnp.concatenate([before, both, after], 1)
    along_y = (rimmed[:, 2:] - rimmed[:, :-2]) * 0.5
    continuity = roll_diff(east_wind, 1) + along_y[0] + upward - below
    balance_x = turning * north_wind - roll_diff(geopotential, 1)
    balance_y = turning * east_wind + along_y[1]
    return jnp.stack([continuity, balance_x, balance_y], 0)


def on_device(forcing, spectral_weight, point_weight, point_bias, decoder, coriolis, layer_depth):
    source = forcing[0]
    fwd, inv = (jnp.asarray(v) for v in x_tables())
    ytab = jnp.asarray(y_tables())
    kron, dec = kron_matrices(point_weight, decoder)
    near = first_local(source, fwd)
    state = source
    for iteration in range(ITERS - 1):
        back = mode_step(near, spectral_weight, ytab)
        state, near = middle_local(back, state, source, kron, point_bias, fwd, inv)
    back = mode_step(near, spectral_weight, ytab)
    final, fields = last_local(back, state, source, kron, point_bias, dec, inv)
    residual = residuals(fields, coriolis, layer_depth)
    return final[None], residual[:, None]


def solution(mesh):
    return jax.shard_map(
        on_device,
        mesh=mesh,
        in_specs=(
            P("lev", None, "gy", None),
            P(None, "gy", None, None, None),
            P(),
            P(),
            P(),
            P("gy"),
            P(),
        ),
        out_specs=(P("lev", None, "gy", None), P(None, "lev", "gy", None)),
        check_vma=False,
    )
```

time: 412 us -> 253 us (0.61); the launches traced: 405 us -> 252 us
  Pallas kernels: 0 us -> 175 us
  matrix products: 127 us -> 0 us
  waiting for transfers between devices: 111 us -> 38.6 us
  blocking collectives: 62.7 us -> 0 us
  local copies, waits for them, and re-layouts: 33.9 us -> 10.3 us
  other arithmetic: 27.7 us -> 6.74 us
  starting transfers between devices: 27 us -> 7.16 us
    pallas_call x0 -> x9, Pallas kernels: none -> 175 us  [the longest x3 118 us: mode_step(): pl.pallas_call(mode_body, name='mode_step', in_specs=[pl.BlockSpec(memory...]
    dot_general x13 -> x0, matrix products: 127 us -> none  [the longest x3 53.4 us: on_device(): jnp.einsum('lrcky,rkx->lcyx', own_modes, table_ix, preferred_element_type...]
    all_to_all x4 -> x0, waiting for transfers between devices: 73.3 us -> none  [the longest x3 46.1 us: copy_for_each(): return lax.all_to_all(copies, axis, split_axis=0, concat_axis=0, tiled=True)]
    all_to_all x2 -> x0, blocking collectives: 62.7 us -> none  [on_device(): lax.all_to_all(near_modes, 'gy', split_axis=3, concat_axis=4, tiled=True)]
    all_to_all x4 -> x0, starting transfers between devices: 19.8 us -> none  [the longest x3 11.8 us: copy_for_each(): return lax.all_to_all(copies, axis, split_axis=0, concat_axis=0, tiled=True)]
    another operation x3 -> x0, local copies, waits for them, and re-layouts: 10.1 us -> none
    convert_element_type x3 -> x0, local copies, waits for them, and re-layouts: 9.82 us -> none  [on_device(): near_modes = jnp.einsum('lcyx,rxk->lrcky', current, table_fx, preferred_e...]
    select_n x9 -> x0, other arithmetic: 9.1 us -> none  [the longest x8 9.09 us: hop(): return jnp.where(reached, new, before)]
  transfers between devices with their start and end apart: 8 -> 4, of which waited for: 8 -> 4; matrix products, arithmetic and copies ran while one was open for 12% -> 0% of each run, Pallas kernels for 0% -> 0%
where the time goes in v1:
time: 253 us; the launch traced here: 252 us
  Pallas kernels  175 us (69%)
  waiting for transfers between devices  38.6 us (15%)
  between operations  14.2 us (6%)
  local copies, waits for them, and re-layouts  10.3 us (4%)
  starting transfers between devices  7.16 us (3%)
  other arithmetic  6.74 us (3%)
    pallas_call x3, Pallas kernels, mode_step(): pl.pallas_call(mode_body, name='mode_step', in_specs=[pl.BlockSpec(memory...  118 us
    pallas_call x2, Pallas kernels, middle_local(): pl.pallas_call(middle_body, name='middle_local', grid=(ROWS // YC,), in_s...  30.6 us
    all_gather x1, waiting for transfers between devices, prefix(): everything = lax.all_gather(value, axis)  24.9 us
    pallas_call x1, Pallas kernels, last_local(): pl.pallas_call(last_body, name='last_local', grid=(ROWS // YC,), in_specs...  15.8 us
    unnamed x27, local copies, waits for them, and re-layouts  9.19 us
    pallas_call x1, Pallas kernels, first_local(): pl.pallas_call(first_body, name='first_local', grid=(ROWS // YC,), in_spe...  7.09 us
    ppermute x1, waiting for transfers between devices, residuals(): below = lax.ppermute(upward, 'lev', [(i, i + 1) for i in range(count - 1)])  6.91 us
    ppermute x1, waiting for transfers between devices, residuals(): before = lax.ppermute(both[:, -1:], 'gy', up)  5.61 us
  transfers between devices with their start and end apart: 4, of which 4 were waited for; matrix products, arithmetic and copies ran while one was open for 0% of the time, Pallas kernels for 0%

profile of v1, /device:TPU:2, one launch (start us, length us, event | category | flops | bytes accessed | tf_op | source)
XLA Modules:
  0.0 252.1 jit_solution(5995337018609562768)
XLA Ops:
  7.2 1.4 copy.26
  8.6 7.1 %first_local.1.near_ref = bf16[2,4,96,1024]{3,2,1,0:T(8,128)(2,1)} custom-call(bf16[32,96,1024]{2,1,0:T(8,128)(2,1)} %bitcast.38, bf16[4,1024,256]{2,1,0:T(8,128)(2,1)} %constant.33.clone.fwd_ref), custom_call_target="tpu_custom_call" | custom-call | tf_op jit(solution)/shard_map/first_local/pallas_call | solution.py:167
  15.7 1.4 copy-done.4
  17.1 43.7 %mode_step.3.back_ref = bf16[2,4,96,1024]{3,2,1,0:T(8,128)(2,1)S(1)} custom-call(bf16[2,4,96,1024]{3,2,1,0:T(8,128)(2,1)S(1)} %copy-done.4, bf16[2,8,32,32,128]{4,3,2,1,0:T(8,128)(2,1)S(1)} %copy-done, bf16[2,4,384,256]{3,2,1,0:T(8,128)(2,1)S(1)} %copy-done.2), custom_call_target="tpu_custom_call" | custom-call | tf_op jit(solution)/shard_map/mode_step/pallas_call | solution.py:326
  60.8 1.2 copy-done.5
  62.0 2.3 pointwise_matrix.1.kron_ref
  64.3 15.3 %middle_local.2 = (bf16[32,96,1024]{2,1,0:T(8,128)(2,1)}, bf16[2,4,96,1024]{3,2,1,0:T(8,128)(2,1)}) custom-call(bf16[2,4,96,1024]{3,2,1,0:T(8,128)(2,1)} %copy-done.5, bf16[32,96,1024]{2,1,0:T(8,128)(2,1)} %bitcast.39, bf16[32,96,1024]{2,1,0:T(8,128)(2,1)} %bitcast.40, bf16[512,512]{1,0:T(8,128)(2,1)} %pointwise_matrix.1.kron_ref, f32[32]{0:T(128)} %bias_ref.5, ...), custom_call_target="tpu_custom_call" | custom-call | tf_op jit(solution)/shard_map/middle_local/pallas_call | solution.py:177
  79.6 1.4 copy-done.8
  81.0 36.3 %mode_step.4.back_ref = bf16[2,4,96,1024]{3,2,1,0:T(8,128)(2,1)S(1)} custom-call(bf16[2,4,96,1024]{3,2,1,0:T(8,128)(2,1)S(1)} %copy-done.8, bf16[2,8,32,32,128]{4,3,2,1,0:T(8,128)(2,1)S(1)} %copy-done.1, bf16[2,4,384,256]{3,2,1,0:T(8,128)(2,1)S(1)} %copy-done.2), custom_call_target="tpu_custom_call" | custom-call | tf_op jit(solution)/shard_map/mode_step/pallas_call | solution.py:326
  117.3 1.1 copy-done.6
  118.4 15.3 %middle_local.3 = (bf16[32,96,1024]{2,1,0:T(8,128)(2,1)}, bf16[2,4,96,1024]{3,2,1,0:T(8,128)(2,1)}) custom-call(bf16[2,4,96,1024]{3,2,1,0:T(8,128)(2,1)} %copy-done.6, bf16[32,96,1024]{2,1,0:T(8,128)(2,1)} %get-tuple-element.9.state_ref, bf16[32,96,1024]{2,1,0:T(8,128)(2,1)} %bitcast.41, bf16[512,512]{1,0:T(8,128)(2,1)} %pointwise_matrix.1.kron_ref, ...), custom_call_target="tpu_custom_call" | custom-call | tf_op jit(solution)/shard_map/middle_local/pallas_call | solution.py:177
  133.8 1.4 copy-done.7
  135.2 37.7 %mode_step.5.back_ref = bf16[2,4,96,1024]{3,2,1,0:T(8,128)(2,1)S(1)} custom-call(bf16[2,4,96,1024]{3,2,1,0:T(8,128)(2,1)S(1)} %copy-done.7, bf16[2,8,32,32,128]{4,3,2,1,0:T(8,128)(2,1)S(1)} %copy-done.1, bf16[2,4,384,256]{3,2,1,0:T(8,128)(2,1)S(1)} %copy-done.2), custom_call_target="tpu_custom_call" | custom-call | tf_op jit(solution)/shard_map/mode_step/pallas_call | solution.py:326
  172.8 1.3 copy-done.3
  174.1 0.6 dynamic_slice.3
  174.7 1.8 decoder_matrix.1.dec_ref
  176.5 15.8 %last_local.1 = (f32[32,96,1024]{2,1,0:T(8,128)}, f32[4,96,1024]{2,1,0:T(8,128)}) custom-call(bf16[2,4,96,1024]{3,2,1,0:T(8,128)(2,1)} %copy-done.3, bf16[32,96,1024]{2,1,0:T(8,128)(2,1)} %get-tuple-element.11.state_ref, bf16[32,96,1024]{2,1,0:T(8,128)(2,1)} %bitcast.42, bf16[512,512]{1,0:T(8,128)(2,1)} %pointwise_matrix.1.kron_ref, f32[32]{0:T(128)} %bias_ref.5, ...), custom_call_target="tpu_custom_call" | custom-call | tf_op jit(solution)/shard_map/last_local/pallas_call | solution.py:188
  192.3 2.6 %fusion.9 = (f32[1,96,1024]{2,1,0:T(8,128)S(1)}, f32[1,96,1024]{2,1,0:T(8,128)}) fusion(f32[4,96,1024]{2,1,0:T(8,128)} %get-tuple-element.13, f32[]{:T(128)} %bitcast.4), kind=kLoop, calls=%fused_computation.31 | loop fusion | flops 98304 | bytes 1572868 | tf_op jit(solution)/shard_map/unstack | solution.py:390
  194.9 24.9 %all-gather.2.cloned.1.call-done = f32[8,96,1024]{2,1,0:T(8,128)} async-done(((f32[1,96,1024]{2,1,0:T(8,128)}), f32[8,96,1024]{2,1,0:T(8,128)}) %all-gather.2.cloned.1.call-update) | async-done | bytes 3145744 | tf_op jit(solution)/shard_map/all_gather | solution.py:379
  219.8 2.4 select_reduce_fusion
  222.3 5.2 %collective-permute-start = (f32[2,1,1024]{2,1,0:T(1,128)S(1)}, f32[2,1,1024]{2,1,0:T(1,128)S(1)}, u32[]{:S(2)}, u32[]{:S(2)}) collective-permute-start(f32[2,1,1024]{2,1,0:T(1,128)S(1)} %get-tuple-element.26), channel_id=1, source_target_pairs={{1,0},{2,1},{3,2},{4,3},{5,4},{6,5},{7,6},{8,7},{9,8},{10,9},{11,1... | collective-permute-start | bytes 24584 | tf_op jit(solution)/shard_map/ppermute | solution.py:401
  227.5 0.2 slice_bitcast_fusion
  227.7 0.1 slice_bitcast_fusion.5
  227.7 1.1 collective-permute-done
  228.9 5.6 %collective-permute-done.1 = f32[2,1,1024]{2,1,0:T(1,128)S(1)} collective-permute-done((f32[2,1,1024]{2,1,0:T(1,128)S(1)}, f32[2,1,1024]{2,1,0:T(1,128)S(1)}, u32[]{:S(2)}, u32[]{:S(2)}) %collective-permute-start.1) | collective-permute-done | bytes 8224 | tf_op jit(solution)/shard_map/ppermute | solution.py:400
  234.5 0.2 fusion.1
  234.7 0.2 fusion.8
  234.9 1.9 collective-permute-start.2
  236.9 0.2 fusion.11
  237.1 6.9 %collective-permute-done.2 = f32[96,1024]{1,0:T(8,128)S(1)} collective-permute-done((f32[96,1024]{1,0:T(8,128)S(1)}, f32[96,1024]{1,0:T(8,128)S(1)}, u32[]{:S(2)}, u32[]{:S(2)}) %collective-permute-start.2) | collective-permute-done | bytes 393248 | tf_op jit(solution)/shard_map/ppermute | solution.py:395
  244.0 0.2 fusion.5
  244.2 1.1 maximum_bitcast_fusion
  (28 shorter events, 0.3 us)
Async XLA Ops:
  7.2 212.6 %all-gather.2.cloned.1.call-start = ((), (), s32[]{:S(2)}) async-start(), calls=%async_computation | async-start | bytes 3538944 | tf_op jit(solution)/shard_map/all_gather | solution.py:379
  8.6 7.1 %copy-start = (bf16[2,8,32,32,128]{4,3,2,1,0:T(8,128)(2,1)S(1)}, bf16[2,8,32,32,128]{4,3,2,1,0:T(8,128)(2,1)}, u32[]{:S(2)}) copy-start(bf16[2,8,32,32,128]{4,3,2,1,0:T(8,128)(2,1)} %weight_ref.5) | copy-start | bytes 12582916
  8.6 7.1 %copy-start.2 = (bf16[2,4,384,256]{3,2,1,0:T(8,128)(2,1)S(1)}, bf16[2,4,384,256]{3,2,1,0:T(8,128)(2,1)}, u32[]{:S(2)}) copy-start(bf16[2,4,384,256]{3,2,1,0:T(8,128)(2,1)} %constant.35.clone.ytab_ref) | copy-start | bytes 4718596
  15.7 1.4 copy-start.4
  60.8 1.2 copy-start.5
  64.3 15.3 %copy-start.1 = (bf16[2,8,32,32,128]{4,3,2,1,0:T(8,128)(2,1)S(1)}, bf16[2,8,32,32,128]{4,3,2,1,0:T(8,128)(2,1)}, u32[]{:S(2)}) copy-start(bf16[2,8,32,32,128]{4,3,2,1,0:T(8,128)(2,1)} %weight_ref.5) | copy-start | bytes 12582916
  79.6 1.4 copy-start.8
  117.3 1.2 copy-start.6
  133.8 1.4 copy-start.7
  135.2 38.9 %copy-start.12 = (f32[8]{0:T(128)S(1)}, f32[8]{0:T(128)}, u32[]{:S(2)}) copy-start(f32[8]{0:T(128)} %param.22) | copy-start | bytes 100
  172.8 1.3 copy-start.3
  194.9 27.3 %copy-start.9 = (f32[1,96,1024]{2,1,0:T(8,128)S(1)}, f32[1,96,1024]{2,1,0:T(8,128)}, u32[]{:S(2)}) copy-start(f32[1,96,1024]{2,1,0:T(8,128)} %get-tuple-element.25) | copy-start | bytes 1179652
  222.3 6.6 %collective-permute-start = (f32[2,1,1024]{2,1,0:T(1,128)S(1)}, f32[2,1,1024]{2,1,0:T(1,128)S(1)}, u32[]{:S(2)}, u32[]{:S(2)}) collective-permute-start(f32[2,1,1024]{2,1,0:T(1,128)S(1)} %get-tuple-element.26), channel_id=1, source_target_pairs={{1,0},{2,1},{3,2},{4,3},{5,4},{6,5},{7,6},{8,7},{9,8},{10,9},{11,1... | collective-permute-start | bytes 24584 | tf_op jit(solution)/shard_map/ppermute | solution.py:401
  227.5 7.2 %copy-start.10 = (f32[4,96,1024]{2,1,0:T(8,128)S(1)}, f32[4,96,1024]{2,1,0:T(8,128)}, u32[]{:S(2)}) copy-start(f32[4,96,1024]{2,1,0:T(8,128)} %get-tuple-element.13) | copy-start | bytes 4718596
  227.5 7.2 %copy-start.11 = (f32[96]{0:T(128)S(1)}, f32[96]{0:T(128)}, u32[]{:S(2)}) copy-start(f32[96]{0:T(128)} %param.21) | copy-start | bytes 1156
  227.5 7.0 %collective-permute-start.1 = (f32[2,1,1024]{2,1,0:T(1,128)S(1)}, f32[2,1,1024]{2,1,0:T(1,128)S(1)}, u32[]{:S(2)}, u32[]{:S(2)}) collective-permute-start(f32[2,1,1024]{2,1,0:T(1,128)S(1)} %get-tuple-element.27), channel_id=1, source_target_pairs={{0,1},{1,2},{2,3},{3,4},{4,5},{5,6},{6,7},{7,8},{8,9},{9,10},{10,1... | collective-permute-start | bytes 24584 | tf_op jit(solution)/shard_map/ppermute | solution.py:400
  234.9 9.1 %collective-permute-start.2 = (f32[96,1024]{1,0:T(8,128)S(1)}, f32[96,1024]{1,0:T(8,128)S(1)}, u32[]{:S(2)}, u32[]{:S(2)}) collective-permute-start(f32[96,1024]{1,0:T(8,128)S(1)} %get-tuple-element.23), channel_id=1, source_target_pairs={{0,16},{16,32},{32,48},{48,64},{64,80},{80,96},{96,112},{1,17},{17... | collective-permute-start | bytes 1179656 | tf_op jit(solution)/shard_map/ppermute | solution.py:395
Sparse Core Ops, SparseCore 0:
  195.0 24.7 all-gather.1

commit v2 on v1

--- a/solution.py
+++ b/solution.py
@@ -348,6 +348,143 @@
     )(near, weights, ytab)
 
 
+def shifted(field, step, axis):
+    return pltpu.roll(field, step % field.shape[axis], axis)
+
+
+def diff_x(field):
+    return (shifted(field, -1, 1) - shifted(field, 1, 1)) * 0.5
+
+
+def diff_y(field, before, after):
+    at = lax.broadcasted_iota(jnp.int32, field.shape, 0)
+    upper = jnp.where(at == field.shape[0] - 1, after, shifted(field, -1, 0))
+    lower = jnp.where(at == 0, before, shifted(field, 1, 0))
+    return (upper - lower) * 0.5
+
+
+def tail_body(fields_ref, turning_ref, depth_ref, out_ref, own, other, chip, lower, total, share, up_out, up_in,
+              geo, edge_out, edge_in, ss, rs):
+    lev = lax.axis_index("lev")
+    g = lax.axis_index("gy")
+    x, c = lev // 2, lev % 2
+    partner = {"lev": 2 * x + 1 - c}
+    next_row, last_row = {"gy": (g + 1) % 16}, {"gy": (g + 15) % 16}
+    beside = {"lev": (lev + 1 + 6 * (1 - c)) % 8}
+    barrier = pltpu.get_barrier_semaphore()
+    for peer in [partner, beside, next_row, last_row] + [{"lev": (lev + 2 * d) % 8} for d in range(1, 4)]:
+        pl.semaphore_signal(barrier, 1, device_id=peer, device_id_type=MESH)
+
+    def copy(src, dst, at, peer):
+        return pltpu.make_async_remote_copy(src_ref=src, dst_ref=dst, send_sem=ss.at[at], recv_sem=rs.at[at],
+                                            device_id=peer, device_id_type=MESH)
+
+    half = pl.ds(pl.multiple_of(48 * c, 48), 48)
+    rest = pl.ds(pl.multiple_of(48 * (1 - c), 48), 48)
+    weighted = fields_ref[3] * depth_ref[lev]
+    own[...] = weighted.astype(BF)
+    up_out[...] = fields_ref[2].astype(BF)
+    edge_out[0] = fields_ref[1, 88:96]
+    edge_out[1] = fields_ref[1, 0:8]
+    pl.semaphore_wait(barrier, 7)
+    all_rows = copy(own, other, 0, partner)
+    some_rows = copy(own.at[0:48], other.at[0:48], 0, partner)
+
+    @pl.when(c == 0)
+    def _():
+        all_rows.start()
+
+    @pl.when(c == 1)
+    def _():
+        some_rows.start()
+
+    winds = [copy(edge_out.at[0], edge_in.at[0], 1, next_row), copy(edge_out.at[1], edge_in.at[1], 2, last_row)]
+    for w in winds:
+        w.start()
+
+    @pl.when(c == 0)
+    def _():
+        all_rows.wait_send()
+        some_rows.wait_recv()
+
+    @pl.when(c == 1)
+    def _():
+        some_rows.wait_send()
+        all_rows.wait_recv()
+
+    chip[...] = (own[half, :].astype(F32) + other[half, :].astype(F32)).astype(BF)
+    sums = [copy(chip, lower.at[d - 1], 2 + d, {"lev": (lev + 2 * d) % 8}) for d in range(1, 4)]
+    for d in range(1, 4):
+        @pl.when(x + d <= 3)
+        def _():
+            sums[d - 1].start()
+
+    rising = copy(up_out, up_in, 6, {"lev": (lev + 1) % 8})
+
+    @pl.when(lev < 7)
+    def _():
+        rising.start()
+
+    for w in winds:
+        w.wait()
+    east, north = fields_ref[0], fields_ref[1]
+    out_ref[0] = diff_x(east) + diff_y(north, edge_in[0, 7:8], edge_in[1, 0:1]) + fields_ref[2]
+    total[half, :] = jnp.zeros((48, NX), F32)
+    for d in range(1, 4):
+        @pl.when(x >= d)
+        def _():
+            sums[d - 1].wait_recv()
+            total[half, :] += lower[d - 1].astype(F32)
+
+    share[...] = total[half, :]
+    shared = copy(share, total.at[half], 7, partner)
+    shared.start()
+
+    @pl.when(lev >= 1)
+    def _():
+        rising.wait_recv()
+        out_ref[0] -= up_in[...].astype(F32)
+
+    shared.wait()
+    geo[...] = total[...] + fields_ref[3] * depth_ref[lev]
+
+    @pl.when(c == 1)
+    def _():
+        geo[...] += other[...].astype(F32)
+
+    edges = [copy(geo.at[88:96], edge_in.at[2], 8, next_row), copy(geo.at[0:8], edge_in.at[3], 9, last_row)]
+    for e in edges:
+        e.start()
+    out_ref[1] = turning_ref[...] * north - diff_x(geo[...])
+    for e in edges:
+        e.wait()
+    out_ref[2] = turning_ref[...] * east + diff_y(geo[...], edge_in[2, 7:8], edge_in[3, 0:1])
+    for d in range(1, 4):
+        @pl.when(x + d <= 3)
+        def _():
+            sums[d - 1].wait_send()
+
+    @pl.when(lev < 7)
+    def _():
+        rising.wait_send()
+
+
+def tail_step(fields, coriolis, layer_depth):
+    vmem = pl.BlockSpec(memory_space=pltpu.VMEM)
+    rows = (ROWS, NX)
+    return pl.pallas_call(
+        tail_body, name="tail_step", in_specs=[vmem, vmem, SMEM], out_specs=vmem,
+        out_shape=jax.ShapeDtypeStruct((3, *rows), F32),
+        scratch_shapes=[
+            pltpu.VMEM(rows, BF), pltpu.VMEM(rows, BF), pltpu.VMEM((48, NX), BF), pltpu.VMEM((3, 48, NX), BF),
+            pltpu.VMEM(rows, F32), pltpu.VMEM((48, NX), F32), pltpu.VMEM(rows, BF), pltpu.VMEM(rows, BF),
+            pltpu.VMEM(rows, F32), pltpu.VMEM((2, 8, NX), F32), pltpu.VMEM((4, 8, NX), F32),
+            pltpu.SemaphoreType.DMA((10,)), pltpu.SemaphoreType.DMA((10,)),
+        ],
+        compiler_params=pltpu.CompilerParams(collective_id=2, has_side_effects=True, vmem_limit_bytes=24 << 20),
+    )(fields, coriolis[:, None], layer_depth)
+
+
 def kron_body(row_ref, wt_ref, col_ref, mask_ref, out_ref):
     left = jnp.dot(row_ref[...], wt_ref[...], preferred_element_type=F32).astype(BF)
     full = jnp.dot(left, col_ref[...], preferred_element_type=F32)
@@ -372,39 +509,6 @@
         return pl.pallas_call(kron_body, name=name, out_shape=jax.ShapeDtypeStruct(m.shape, BF))(a, w, b, m)
 
     return call("pointwise_matrix", rows, point_weight.T, cols, mask), call("decoder_matrix", dec_rows, decoder, dec_cols, dec_mask)
-
-
-def prefix(value, axis):
-    peers, place = lax.axis_size(axis), lax.axis_index(axis)
-    everything = lax.all_gather(value, axis)
-    kept = jnp.where((jnp.arange(peers) < place)[:, None, None], everything, 0.0)
-    return jnp.sum(kept, 0)
-
-
-def roll_diff(field, axis):
-    return (jnp.roll(field, -1, axis) - jnp.roll(field, 1, axis)) * 0.5
-
-
-def residuals(fields, coriolis, layer_depth):
-    turning = coriolis[:, None]
-    east_wind, north_wind, upward, heat = fields
-    own_depth = lax.dynamic_slice_in_dim(layer_depth, lax.axis_index("lev"), 1, 0)
-    inside = own_depth[:, None] * heat
-    geopotential = inside + prefix(inside, "lev")
-    count = lax.axis_size("lev")
-    below = lax.ppermute(upward, "lev", [(i, i + 1) for i in range(count - 1)])
-    peers = lax.axis_size("gy")
-    up = [(i, (i + 1) % peers) for i in range(peers)]
-    down = [(j, i) for i, j in up]
-    both = jnp.stack([north_wind, geopotential], 0)
-    before = lax.ppermute(both[:, -1:], "gy", up)
-    after = lax.ppermute(both[:, :1], "gy", down)
-    rimmed = jnp.concatenate([before, both, after], 1)
-    along_y = (rimmed[:, 2:] - rimmed[:, :-2]) * 0.5
-    continuity = roll_diff(east_wind, 1) + along_y[0] + upward - below
-    balance_x = turning * north_wind - roll_diff(geopotential, 1)
-    balance_y = turning * east_wind + along_y[1]
-    return jnp.stack([continuity, balance_x, balance_y], 0)
 
 
 def on_device(forcing, spectral_weight, point_weight, point_bias, decoder, coriolis, layer_depth):
@@ -419,7 +523,7 @@
         state, near = middle_local(back, state, source, kron, point_bias, fwd, inv)
     back = mode_step(near, spectral_weight, ytab)
     final, fields = last_local(back, state, source, kron, point_bias, dec, inv)
-    residual = residuals(fields, coriolis, layer_depth)
+    residual = tail_step(fields, coriolis, layer_depth)
     return final[None], residual[:, None]
 
 

time: 253 us -> 205 us (0.81)
  waiting for transfers between devices: 38.6 us -> 0 us
  Pallas kernels: 175 us -> 193 us
  between operations: 14.2 us -> 0.73 us
  starting transfers between devices: 7.16 us -> 0 us
  other arithmetic: 6.74 us -> 0 us
    all_gather x1 -> x0, waiting for transfers between devices: 24.9 us -> none  [prefix(): everything = lax.all_gather(value, axis)]
    pallas_call x0 -> x1, Pallas kernels: none -> 17.4 us  [tail_step(): pl.pallas_call(tail_body, name='tail_step', in_specs=[vmem, vmem, SMEM],...]
    ppermute x3 -> x0, waiting for transfers between devices: 13.6 us -> none  [the longest x1 6.91 us: residuals(): below = lax.ppermute(upward, 'lev', [(i, i + 1) for i in range(count - 1)])]
    ppermute x3 -> x0, starting transfers between devices: 7.12 us -> none  [the longest x1 5.19 us: residuals(): after = lax.ppermute(both[:, :1], 'gy', down)]
    another operation x2 -> x0, other arithmetic: 2.76 us -> none  [the longest x1 2.55 us: residuals(): east_wind, north_wind, upward, heat = fields]
    unnamed x27 -> x28, local copies, waits for them, and re-layouts: 9.19 us -> 10.8 us
  transfers between devices with their start and end apart: 4 -> 0, of which waited for: 4 -> 0; matrix products, arithmetic and copies ran while one was open for 0% -> 0% of each run, Pallas kernels for 0% -> 0%
where the time goes in v2:
time: 205 us; the launch traced here: 204 us
  Pallas kernels  193 us (94%)
  local copies, waits for them, and re-layouts  10.9 us (5%)
    pallas_call x3, Pallas kernels, mode_step(): pl.pallas_call(mode_body, name='mode_step', in_specs=[pl.BlockSpec(memory...  118 us
    pallas_call x2, Pallas kernels, middle_local(): pl.pallas_call(middle_body, name='middle_local', grid=(ROWS // YC,), in_s...  30.5 us
    pallas_call x1, Pallas kernels, tail_step(): pl.pallas_call(tail_body, name='tail_step', in_specs=[vmem, vmem, SMEM],...  17.4 us
    pallas_call x1, Pallas kernels, last_local(): pl.pallas_call(last_body, name='last_local', grid=(ROWS // YC,), in_specs...  16 us
    unnamed x28, local copies, waits for them, and re-layouts  10.8 us
    pallas_call x1, Pallas kernels, first_local(): pl.pallas_call(first_body, name='first_local', grid=(ROWS // YC,), in_spe...  7.07 us
    pallas_call x2, Pallas kernels, call(): pl.pallas_call(kron_body, name=name, out_shape=jax.ShapeDtypeStruct(m.sha...  4.1 us

profile of v2, /device:TPU:2, one launch (start us, length us, event | category | flops | bytes accessed | tf_op | source)
XLA Modules:
  0.0 204.2 jit_solution(10619285224000478926)
XLA Ops:
  0.6 0.0 copy-start
  0.6 0.0 copy-start.2
  0.7 7.1 %first_local.1.near_ref = bf16[2,4,96,1024]{3,2,1,0:T(8,128)(2,1)} custom-call(bf16[32,96,1024]{2,1,0:T(8,128)(2,1)} %bitcast.8, bf16[4,1024,256]{2,1,0:T(8,128)(2,1)} %constant.18.clone.fwd_ref), custom_call_target="tpu_custom_call" | custom-call | tf_op jit(solution)/shard_map/first_local/pallas_call | solution.py:167
  7.7 0.0 copy-done
  7.7 0.0 copy-done.2
  7.7 1.4 copy-done.4
  9.1 43.7 %mode_step.3.back_ref = bf16[2,4,96,1024]{3,2,1,0:T(8,128)(2,1)S(1)} custom-call(bf16[2,4,96,1024]{3,2,1,0:T(8,128)(2,1)S(1)} %copy-done.4, bf16[2,8,32,32,128]{4,3,2,1,0:T(8,128)(2,1)S(1)} %copy-done, bf16[2,4,384,256]{3,2,1,0:T(8,128)(2,1)S(1)} %copy-done.2), custom_call_target="tpu_custom_call" | custom-call | tf_op jit(solution)/shard_map/mode_step/pallas_call | solution.py:326
  52.8 0.0 copy-start.5
  52.8 1.2 copy-done.5
  54.0 0.0 copy-done.11
  54.0 0.7 copy.18
  54.7 2.3 %pointwise_matrix.1.kron_ref = bf16[512,512]{1,0:T(8,128)(2,1)} custom-call(bf16[512,32]{1,0:T(8,128)(2,1)} %constant.21.clone.row_ref, bf16[32,32]{1,0:T(8,128)(2,1)} %bitcast.13, bf16[32,512]{1,0:T(8,128)(2,1)} %constant.22.clone.col_ref, bf16[512,512]{1,0:T(8,128)(2,1)} %constant.23.clone.mask_ref), custom_call_target="tpu_custom_call" | custom-call | tf_op jit(solution)/shard_map/pointwise_matrix/pallas_call | solution.py:509
  57.0 15.3 %middle_local.2 = (bf16[32,96,1024]{2,1,0:T(8,128)(2,1)}, bf16[2,4,96,1024]{3,2,1,0:T(8,128)(2,1)}) custom-call(bf16[2,4,96,1024]{3,2,1,0:T(8,128)(2,1)} %copy-done.5, bf16[32,96,1024]{2,1,0:T(8,128)(2,1)} %bitcast.9, bf16[32,96,1024]{2,1,0:T(8,128)(2,1)} %bitcast.10, bf16[512,512]{1,0:T(8,128)(2,1)} %pointwise_matrix.1.kron_ref, f32[32]{0:T(128)} %bias_ref.5, ...), custom_call_target="tpu_custom_call" | custom-call | tf_op jit(solution)/shard_map/middle_local/pallas_call | solution.py:177
  72.3 0.0 copy-done.1
  72.3 1.4 copy-done.9
  73.7 36.3 %mode_step.4.back_ref = bf16[2,4,96,1024]{3,2,1,0:T(8,128)(2,1)S(1)} custom-call(bf16[2,4,96,1024]{3,2,1,0:T(8,128)(2,1)S(1)} %copy-done.9, bf16[2,8,32,32,128]{4,3,2,1,0:T(8,128)(2,1)S(1)} %copy-done.1, bf16[2,4,384,256]{3,2,1,0:T(8,128)(2,1)S(1)} %copy-done.2), custom_call_target="tpu_custom_call" | custom-call | tf_op jit(solution)/shard_map/mode_step/pallas_call | solution.py:326
  110.0 0.0 copy-start.6
  110.0 1.1 copy-done.6
  111.2 15.2 %middle_local.3 = (bf16[32,96,1024]{2,1,0:T(8,128)(2,1)}, bf16[2,4,96,1024]{3,2,1,0:T(8,128)(2,1)}) custom-call(bf16[2,4,96,1024]{3,2,1,0:T(8,128)(2,1)} %copy-done.6, bf16[32,96,1024]{2,1,0:T(8,128)(2,1)} %get-tuple-element.9.state_ref, bf16[32,96,1024]{2,1,0:T(8,128)(2,1)} %bitcast.11, bf16[512,512]{1,0:T(8,128)(2,1)} %pointwise_matrix.1.kron_ref, ...), custom_call_target="tpu_custom_call" | custom-call | tf_op jit(solution)/shard_map/middle_local/pallas_call | solution.py:177
  126.3 1.4 copy-done.8
  127.7 37.7 %mode_step.5.back_ref = bf16[2,4,96,1024]{3,2,1,0:T(8,128)(2,1)S(1)} custom-call(bf16[2,4,96,1024]{3,2,1,0:T(8,128)(2,1)S(1)} %copy-done.8, bf16[2,8,32,32,128]{4,3,2,1,0:T(8,128)(2,1)S(1)} %copy-done.1, bf16[2,4,384,256]{3,2,1,0:T(8,128)(2,1)S(1)} %copy-done.2), custom_call_target="tpu_custom_call" | custom-call | tf_op jit(solution)/shard_map/mode_step/pallas_call | solution.py:326
  165.4 0.0 copy-start.3
  165.4 1.1 copy-done.3
  166.6 1.8 decoder_matrix.1.dec_ref
  168.4 16.0 %last_local.1 = (f32[32,96,1024]{2,1,0:T(8,128)}, f32[4,96,1024]{2,1,0:T(8,128)}) custom-call(bf16[2,4,96,1024]{3,2,1,0:T(8,128)(2,1)} %copy-done.3, bf16[32,96,1024]{2,1,0:T(8,128)(2,1)} %get-tuple-element.11.state_ref, bf16[32,96,1024]{2,1,0:T(8,128)(2,1)} %bitcast.12, bf16[512,512]{1,0:T(8,128)(2,1)} %pointwise_matrix.1.kron_ref, f32[32]{0:T(128)} %bias_ref.5, ...), custom_call_target="tpu_custom_call" | custom-call | tf_op jit(solution)/shard_map/last_local/pallas_call | solution.py:188
  184.3 0.0 copy-done.12
  184.3 0.1 copy.19.turning_ref
  184.4 0.0 copy-done.10
  184.4 0.0 copy-start.7
  184.4 1.4 copy-done.7
  185.8 17.4 %tail_step.1 = f32[3,96,1024]{2,1,0:T(8,128)S(1)} custom-call(f32[4,96,1024]{2,1,0:T(8,128)S(1)} %copy-done.7, f32[96,1]{1,0:T(8,128)S(1)} %copy.19.turning_ref, f32[8]{0:T(128)S(1)} %copy-done.10), custom_call_target="tpu_custom_call" | custom-call | tf_op jit(solution)/shard_map/tail_step/pallas_call | solution.py:475
  203.2 1.0 copy.22
  (7 shorter events, 0.0 us)
Async XLA Ops:
  0.6 7.1 %copy-start = (bf16[2,8,32,32,128]{4,3,2,1,0:T(8,128)(2,1)S(1)}, bf16[2,8,32,32,128]{4,3,2,1,0:T(8,128)(2,1)}, u32[]{:S(2)}) copy-start(bf16[2,8,32,32,128]{4,3,2,1,0:T(8,128)(2,1)} %weight_ref.5) | copy-start | bytes 12582916
  0.6 7.1 %copy-start.2 = (bf16[2,4,384,256]{3,2,1,0:T(8,128)(2,1)S(1)}, bf16[2,4,384,256]{3,2,1,0:T(8,128)(2,1)}, u32[]{:S(2)}) copy-start(bf16[2,4,384,256]{3,2,1,0:T(8,128)(2,1)} %constant.20.clone.ytab_ref) | copy-start | bytes 4718596
  7.7 1.4 copy-start.4
  9.1 44.8 %copy-start.11 = (bf16[32,32]{1,0:T(8,128)(2,1)S(1)}, bf16[32,32]{1,0:T(8,128)(2,1)}, u32[]{:S(2)}) copy-start(bf16[32,32]{1,0:T(8,128)(2,1)} %param.18) | copy-start | bytes 6148
  52.8 1.2 copy-start.5
  57.0 15.3 %copy-start.1 = (bf16[2,8,32,32,128]{4,3,2,1,0:T(8,128)(2,1)S(1)}, bf16[2,8,32,32,128]{4,3,2,1,0:T(8,128)(2,1)}, u32[]{:S(2)}) copy-start(bf16[2,8,32,32,128]{4,3,2,1,0:T(8,128)(2,1)} %weight_ref.5) | copy-start | bytes 12582916
  72.3 1.4 copy-start.9
  110.0 1.1 copy-start.6
  126.3 1.4 copy-start.8
  165.4 1.1 copy-start.3
  168.4 16.0 %copy-start.12 = (f32[96]{0:T(128)S(1)}, f32[96]{0:T(128)}, u32[]{:S(2)}) copy-start(f32[96]{0:T(128)} %param.21) | copy-start | bytes 1156
  168.4 16.1 %copy-start.10 = (f32[8]{0:T(128)S(1)}, f32[8]{0:T(128)}, u32[]{:S(2)}) copy-start(f32[8]{0:T(128)} %depth_ref.1) | copy-start | bytes 100
  184.4 1.4 copy-start.7

commit v3 on v2

v3 whole, which is shorter than its diff:
```python
import functools
import math

import jax
import jax.numpy as jnp
import numpy as np
from jax import lax
from jax.experimental import pallas as pl
from jax.experimental.pallas import tpu as pltpu
from jax.sharding import PartitionSpec as P

C = 32
NX = 1024
NY = 1536
M = 128
ROWS = 96
ITERS = 3
MESH = pl.DeviceIdType.MESH
BF = jnp.bfloat16
F32 = jnp.float32
YC = 32
TILE = 256


def turns(a, b, length):
    phase = (a[:, None] * b[None, :]) % length
    return phase.astype(np.float32) * np.float32(2.0 * math.pi / length)


def lane_modes(half, order):
    p, r, s, j = np.meshgrid(np.array(order), np.arange(2), np.arange(4), np.arange(8), indexing="ij")
    k = 32 * s + 8 * p + j if half == 0 else 32 * p + 8 * s + j
    return k.reshape(-1), r.reshape(-1)


@functools.lru_cache(None)
def x_tables():
    forward, inverse = [], []
    for half in range(2):
        for order in ((0, 1, 2, 3), (1, 0, 3, 2)):
            k, r = lane_modes(half, order)
            turned = turns(np.arange(NX), k, NX)
            wave = np.where(r == 0, np.cos(turned), -np.sin(turned)).astype(np.float32)
            factor = np.where(k == 0, 1.0, 2.0).astype(np.float32) / np.float32(NX * NY)
            forward.append(wave)
            inverse.append((wave * factor[None, :]).T)
    return np.stack(forward).astype(BF), np.stack(inverse).astype(BF)


@functools.lru_cache(None)
def y_tables():
    m = np.arange(M)
    signed = np.where(m < M // 2, m, m + NY - M)
    rows = np.arange(NY)
    turned = turns(rows, signed, NY)
    both = np.concatenate([np.cos(turned), np.sin(turned)], 1).astype(np.float32).astype(BF)
    blocks = both.reshape(4, 4, ROWS, 2 * M)
    first = blocks.reshape(4, 4 * ROWS, 2 * M)
    second = blocks.transpose(1, 0, 2, 3).reshape(4, 4 * ROWS, 2 * M)
    return np.stack([first, second])


def gelu(v):
    inner = v * (math.sqrt(2.0 / math.pi) + (math.sqrt(2.0 / math.pi) * 0.044715) * (v * v))
    return (0.5 * v) * (1.0 + jnp.tanh(inner))


def lane_mask(rows):
    return lax.broadcasted_iota(jnp.int32, (rows, 128), 1) < 64


def update_chunk(back_ref, state_ref, forcing_ref, kron_ref, bias_ref, inv_ref, sink, yc):
    mask = lane_mask(yc)
    groups = []
    for h in range(2):
        even, odd = [], []
        for pair in range(8):
            b = [back_ref[h, p, :, 128 * pair:128 * pair + 128] for p in range(4)]
            even.append(jnp.concatenate([jnp.where(mask, b[0], b[1]), jnp.where(mask, b[2], b[3])], 1))
            odd.append(jnp.concatenate([jnp.where(mask, b[1], b[0]), jnp.where(mask, b[3], b[2])], 1))
        groups.append(jnp.concatenate(even, 0))
        groups.append(jnp.concatenate(odd, 0))
    for t in range(NX // TILE):
        cols = slice(t * TILE, (t + 1) * TILE)
        mixed = []
        for s in range(yc // 16):
            st = state_ref[:, 16 * s:16 * s + 16, cols].reshape(C * 16, TILE)
            mixed.append(jnp.dot(kron_ref[...], st, preferred_element_type=F32).reshape(4, 8, 16, TILE))
        for g in range(4):
            h, par = g // 2, g % 2
            spread = jnp.dot(groups[g], inv_ref[g, :, cols], preferred_element_type=F32)
            spread = spread.reshape(8, yc, TILE)
            for pair in range(8):
                c = 16 * h + 2 * pair + par
                pw = jnp.concatenate([m[g, pair] for m in mixed], 0)
                v = spread[pair] + pw + (forcing_ref[c, :, cols].astype(F32) + bias_ref[c])
                sink(g, pair, c, cols, gelu(v))


def last_body(back_ref, state_ref, forcing_ref, pick_ref, wt_ref, cols_ref, bias_ref, four_ref, dec_ref, dcols_ref, inv_ref,
              out_ref, fields_ref, hold, kron_ref, dmat_ref):
    @pl.when(pl.program_id(0) == 0)
    def _():
        kron_ref[...] = kron_values(pick_ref[...], wt_ref[...], cols_ref[...])
        dmat_ref[...] = kron_values(four_ref[...], dec_ref[...], dcols_ref[...])

    def sink(g, pair, c, cols, value):
        out_ref[c, :, cols] = value
        hold[8 * g + pair, :, cols] = value.astype(BF)

    update_chunk(back_ref, state_ref, forcing_ref, kron_ref, bias_ref, inv_ref, sink, YC)
    for s in range(YC // 16):
        rows = hold[:, 16 * s:16 * s + 16, :].reshape(C * 16, NX)
        f = jnp.dot(dmat_ref[...], rows, preferred_element_type=F32)
        fields_ref[:, 16 * s:16 * s + 16, :] = f.reshape(4, 16, NX)


def rows_spec(lead, yc):
    n = len(lead)
    return pl.BlockSpec((*lead, yc, NX), lambda i: (0,) * n + (i, 0))


def whole_spec(shape):
    return pl.BlockSpec(shape, lambda i: (0,) * len(shape), pipeline_mode=pl.Buffered(1))


SMEM = pl.BlockSpec(memory_space=pltpu.SMEM)
LIMIT = 56 << 20


def last_local(back, state, forcing, pick, wt, cols, bias, four, dec, dec_cols, inv):
    return pl.pallas_call(
        last_body, name="last_local", grid=(ROWS // YC,),
        in_specs=[rows_spec((2, 4), YC), rows_spec((C,), YC), rows_spec((C,), YC), whole_spec(pick.shape),
                  whole_spec(wt.shape), whole_spec(cols.shape), SMEM, whole_spec(four.shape), whole_spec(dec.shape),
                  whole_spec(dec_cols.shape), whole_spec(inv.shape)],
        out_specs=[rows_spec((C,), YC), rows_spec((4,), YC)],
        out_shape=[jax.ShapeDtypeStruct((C, ROWS, NX), F32), jax.ShapeDtypeStruct((4, ROWS, NX), F32)],
        scratch_shapes=[pltpu.VMEM((C, YC, NX), BF), pltpu.VMEM((C * 16, C * 16), BF), pltpu.VMEM((64, C * 16), BF)],
        compiler_params=pltpu.CompilerParams(vmem_limit_bytes=LIMIT),
    )(back, state, forcing, pick, wt, cols, bias, four, dec, dec_cols, inv)


def kron_values(rows, weight, cols):
    left = jnp.dot(rows, weight, preferred_element_type=F32).astype(BF)
    full = jnp.dot(left, cols, preferred_element_type=F32)
    i = lax.broadcasted_iota(jnp.int32, full.shape, 0) % 16
    j = lax.broadcasted_iota(jnp.int32, full.shape, 1) % 16
    return jnp.where(i == j, full, 0.0).astype(BF)


def steps_body(forcing_ref, weight_ref, ytab_ref, fwd_hbm, inv_hbm, pick_ref, wt_ref, cols_ref, bias_ref,
               state_out, back_out,
               source, state, fwd, inv, kron, wbuf, tabs, near, r1, part, s2, r2, sp, mx, r3, m2, s4, back,
               lsem, s1s, s1r, s2s, s2r, s3s, s3r, s4s, s4r):
    g = lax.axis_index("gy")
    z, y = g // 4, g % 4
    own = ((y, z), (z, y))

    def first_peer(h, a):
        return {"gy": z * 4 + a} if h == 0 else {"gy": a * 4 + y}

    def second_peer(h, b):
        return {"gy": b * 4 + y} if h == 0 else {"gy": z * 4 + b}

    barrier = pltpu.get_barrier_semaphore()
    for h in range(2):
        for d in range(1, 4):
            pl.semaphore_signal(barrier, 1, device_id=first_peer(h, (own[h][0] + d) % 4), device_id_type=MESH)

    def rows_of(k):
        return pl.ds(pl.multiple_of(k * YC, YC), YC)

    chunks = ROWS // YC

    def local(src, dst, at):
        return pltpu.make_async_copy(src, dst, lsem.at[at])

    load_fwd = local(fwd_hbm, fwd, 0)
    load_source = [local(forcing_ref.at[:, rows_of(k)], source.at[:, rows_of(k)], 1 + k) for k in range(chunks)]
    load_tabs = [local(ytab_ref.at[h, own[h][1]], tabs.at[h], 4 + h) for h in range(2)]
    load_weights = local(weight_ref, wbuf, 6)
    load_inv = local(inv_hbm, inv, 7)
    load_state = local(forcing_ref, state, 8)
    for c in [load_fwd, *load_source, *load_tabs, load_weights, load_inv, load_state]:
        c.start()

    def remote(src, dst, send, recv, peer):
        return pltpu.make_async_remote_copy(src_ref=src, dst_ref=dst, send_sem=send, recv_sem=recv, device_id=peer,
                                            device_id_type=MESH)

    def one(h, d, k):
        a = own[h][0]
        return remote(near.at[h, (a + d) % 4, rows_of(k)], r1.at[h, a, rows_of(k)], s1s.at[h, d - 1, k],
                      s1r.at[h, d - 1, k], first_peer(h, (a + d) % 4))

    def two(h, d):
        b = own[h][1]
        return remote(s2.at[h, (b + d) % 4], r2.at[h, d - 1], s2s.at[h, d - 1], s2r.at[h, d - 1],
                      second_peer(h, (b + d) % 4))

    def three(h, d):
        b = own[h][1]
        return remote(r3.at[h, b], r3.at[h, b], s3s.at[h, d - 1], s3r.at[h, d - 1], second_peer(h, (b + d) % 4))

    def four(h, d, k):
        a = own[h][0]
        return remote(s4.at[h, (a + d) % 4, rows_of(k)], back.at[h, a, rows_of(k)], s4s.at[h, d - 1, k],
                      s4r.at[h, d - 1, k], first_peer(h, (a + d) % 4))

    def forward(k, load):
        rows = rows_of(k)
        mask = lane_mask(YC)
        for h in range(2):
            outs = []
            for par in range(2):
                lhs = jnp.concatenate([load(16 * h + 2 * pair + par, rows) for pair in range(8)], 0)
                outs.append(jnp.dot(lhs, fwd[2 * h + par], preferred_element_type=F32))
            even, odd = outs
            for pair in range(8):
                at = slice(pair * YC, (pair + 1) * YC)
                for v in range(2):
                    e = even[at, 128 * v:128 * v + 128]
                    o = odd[at, 128 * v:128 * v + 128]
                    lanes = slice(128 * pair, 128 * pair + 128)
                    near[h, 2 * v, rows, lanes] = jnp.where(mask, e, o).astype(BF)
                    near[h, 2 * v + 1, rows, lanes] = jnp.where(mask, o, e).astype(BF)
            for d in range(1, 4):
                one(h, d, k).start()
            a = own[h][0]
            r1[h, a, rows] = near[h, a, rows]

    def update(k):
        rows = rows_of(k)
        mask = lane_mask(YC)
        groups = []
        for h in range(2):
            even, odd = [], []
            for pair in range(8):
                b = [back[h, p, rows, 128 * pair:128 * pair + 128] for p in range(4)]
                even.append(jnp.concatenate([jnp.where(mask, b[0], b[1]), jnp.where(mask, b[2], b[3])], 1))
                odd.append(jnp.concatenate([jnp.where(mask, b[1], b[0]), jnp.where(mask, b[3], b[2])], 1))
            groups.append(jnp.concatenate(even, 0))
            groups.append(jnp.concatenate(odd, 0))
        for t in range(NX // TILE):
            cols = slice(t * TILE, (t + 1) * TILE)
            mixed = []
            for s in range(YC // 16):
                at = pl.ds(pl.multiple_of(k * YC + 16 * s, 16), 16)
                st = state[:, at, cols].reshape(C * 16, TILE)
                mixed.append(jnp.dot(kron[...], st, preferred_element_type=F32).reshape(4, 8, 16, TILE))
            for q in range(4):
                h, par = q // 2, q % 2
                spread = jnp.dot(groups[q], inv[q, :, cols], preferred_element_type=F32)
                spread = spread.reshape(8, YC, TILE)
                for pair in range(8):
                    c = 16 * h + 2 * pair + par
                    pw = jnp.concatenate([m[q, pair] for m in mixed], 0)
                    v = spread[pair] + pw + (source[c, rows, cols].astype(F32) + bias_ref[c])
                    state[c, rows, cols] = gelu(v).astype(BF)

    pl.semaphore_wait(barrier, 6)
    load_fwd.wait()
    for k in range(chunks):
        load_source[k].wait()
    pl.loop(0, chunks)(lambda k: forward(k, lambda c, rows: source[c, rows]))
    kron[...] = kron_values(pick_ref[...], wt_ref[...], cols_ref[...])
    for c in [*load_tabs, load_weights, load_inv, load_state]:
        c.wait()

    @pl.loop(0, ITERS)
    def _(it):
        for h in range(2):
            a, b = own[h]
            for k in range(chunks):
                for d in range(1, 4):
                    one(h, d, k).wait()

            @pl.loop(0, 4)
            def _(n):
                cols = pl.ds(pl.multiple_of(n * 256, 256), 256)
                x = r1[h, :, :, cols].reshape(4 * ROWS, 256)
                pt = lax.dot_general(x, tabs[h], (((0,), (0,)), ((), ())), preferred_element_type=F32)
                pt = pt.reshape(2, 2, 2, 4, 8, 256)
                for pair in range(2):
                    for h2 in range(2):
                        q0, q1 = pt[pair, h2, 0], pt[pair, h2, 1]
                        re = q0[..., :M] + q1[..., M:]
                        im = q1[..., :M] - q0[..., M:]
                        both = jnp.concatenate([re, im], 1)
                        c = 2 * (2 * n + pair) + lax.rem(h2 + a, 2)
                        part[h, :, c] = both
                        s2[h, :, c] = both.astype(BF)

            for d in range(1, 4):
                two(h, d).start()
        for h in range(2):
            b = own[h][1]
            for d in range(1, 4):
                two(h, d).wait()

            @pl.loop(0, 16)
            def _(c):
                total = part[h, b, c]
                for d in range(3):
                    total = total + r2[h, d, c].astype(F32)
                sp[16 * h + c] = total

        for oh in range(2):
            b = own[oh][1]
            outs = pl.ds(16 * oh, 16)
            for j in range(8):
                def add(i, acc):
                    ar, ai = acc
                    wr = wbuf[0, j, i, outs].astype(F32)
                    wi = wbuf[1, j, i, outs].astype(F32)
                    sr = jnp.broadcast_to(sp[i, pl.ds(j, 1), :], (16, M))
                    si = jnp.broadcast_to(sp[i, pl.ds(8 + j, 1), :], (16, M))
                    return ar + (sr * wr - si * wi), ai + (sr * wi + si * wr)

                zero = jnp.zeros((16, M), F32)
                ar, ai = lax.fori_loop(0, C, add, (zero, zero), unroll=8)
                mx[pl.ds(j, 16, stride=16), :] = ar
                mx[pl.ds(8 + j, 16, stride=16), :] = ai
            r3[oh, b] = mx[...].reshape(16, 16, M).astype(BF)
            for d in range(1, 4):
                three(oh, d).start()
        for h in range(2):
            a = own[h][0]
            for d in range(1, 4):
                three(h, d).wait()

            @pl.loop(0, 8)
            def _(n):
                rows = []
                for h2 in range(2):
                    c = 2 * n + lax.rem(h2 + a, 2)
                    block = r3[h, :, c].astype(F32).reshape(4, 2, 8, M)
                    re = block[:, 0].reshape(32, M)
                    im = block[:, 1].reshape(32, M)
                    rows.append(jnp.concatenate([re, -im], 1))
                    rows.append(jnp.concatenate([im, re], 1))
                m2[h, pl.ds(pl.multiple_of(n * 128, 128), 128)] = jnp.concatenate(rows, 0).astype(BF)

        @pl.loop(0, chunks)
        def _(k):
            rows = rows_of(k)
            for h in range(2):
                a = own[h][0]
                left = jnp.concatenate([tabs[h, pl.ds(pl.multiple_of(ROWS * p + k * YC, YC), YC)] for p in range(4)], 0)
                for n in range(4):
                    lanes = slice(256 * n, 256 * n + 256)
                    out = lax.dot_general(left, m2[h, lanes], (((1,), (1,)), ((), ())), preferred_element_type=F32)
                    s4[h, :, rows, lanes] = out.reshape(4, YC, 256).astype(BF)
                for d in range(1, 4):
                    four(h, d, k).start()
                back[h, a, rows] = s4[h, a, rows]

        @pl.when(it < ITERS - 1)
        def _():
            @pl.loop(0, chunks)
            def _(k):
                for h in range(2):
                    for d in range(1, 4):
                        four(h, d, k).wait()
                update(k)

                @pl.when(it == ITERS - 2)
                def _():
                    pltpu.make_async_copy(state.at[:, rows_of(k)], state_out.at[:, rows_of(k)], lsem.at[1 + k]).start()

                forward(k, lambda c, rows: state[c, rows])

    for k in range(chunks):
        for h in range(2):
            for d in range(1, 4):
                four(h, d, k).wait()
        pltpu.make_async_copy(back.at[:, :, rows_of(k)], back_out.at[:, :, rows_of(k)], lsem.at[4 + k]).start()
    for k in range(chunks):
        pltpu.make_async_copy(state.at[:, rows_of(k)], state_out.at[:, rows_of(k)], lsem.at[1 + k]).wait()
        pltpu.make_async_copy(back.at[:, :, rows_of(k)], back_out.at[:, :, rows_of(k)], lsem.at[4 + k]).wait()


def steps(forcing, weights, ytab, fwd, inv, pick, wt, cols, bias):
    near_shape = (2, 4, ROWS, NX)
    chunks = ROWS // YC
    any_space = pl.BlockSpec(memory_space=pl.ANY)
    vmem = pl.BlockSpec(memory_space=pltpu.VMEM)
    dma = pltpu.SemaphoreType.DMA
    return pl.pallas_call(
        steps_body, name="steps",
        in_specs=[any_space] * 5 + [vmem] * 3 + [SMEM],
        out_specs=[any_space, any_space],
        out_shape=[jax.ShapeDtypeStruct((C, ROWS, NX), BF), jax.ShapeDtypeStruct(near_shape, BF)],
        scratch_shapes=[
            pltpu.VMEM((C, ROWS, NX), BF),
            pltpu.VMEM((C, ROWS, NX), BF),
            pltpu.VMEM(fwd.shape, BF),
            pltpu.VMEM(inv.shape, BF),
            pltpu.VMEM((C * 16, C * 16), BF),
            pltpu.VMEM((2, 8, C, C, M), BF),
            pltpu.VMEM((2, 4 * ROWS, 2 * M), BF),
            pltpu.VMEM(near_shape, BF),
            pltpu.VMEM(near_shape, BF),
            pltpu.VMEM((2, 4, 16, 16, M), F32),
            pltpu.VMEM((2, 4, 16, 16, M), BF),
            pltpu.VMEM((2, 3, 16, 16, M), BF),
            pltpu.VMEM((C, 16, M), F32),
            pltpu.VMEM((16 * 16, M), F32),
            pltpu.VMEM((2, 4, 16, 16, M), BF),
            pltpu.VMEM((2, NX, 2 * M), BF),
            pltpu.VMEM(near_shape, BF),
            pltpu.VMEM(near_shape, BF),
            dma((9,)),
            dma((2, 3, chunks)), dma((2, 3, chunks)),
            dma((2, 3)), dma((2, 3)), dma((2, 3)), dma((2, 3)),
            dma((2, 3, chunks)), dma((2, 3, chunks)),
        ],
        compiler_params=pltpu.CompilerParams(collective_id=1, has_side_effects=True, vmem_limit_bytes=LIMIT),
    )(forcing, weights, ytab, fwd, inv, pick, wt, cols, bias)


def shifted(field, step, axis):
    return pltpu.roll(field, step % field.shape[axis], axis)


def diff_x(field):
    return (shifted(field, -1, 1) - shifted(field, 1, 1)) * 0.5


def diff_y(field, before, after):
    at = lax.broadcasted_iota(jnp.int32, field.shape, 0)
    upper = jnp.where(at == field.shape[0] - 1, after, shifted(field, -1, 0))
    lower = jnp.where(at == 0, before, shifted(field, 1, 0))
    return (upper - lower) * 0.5


def tail_body(fields_ref, turning_ref, depth_ref, out_ref, own, other, chip, lower, total, share, up_out, up_in,
              geo, edge_out, edge_in, ss, rs):
    lev = lax.axis_index("lev")
    g = lax.axis_index("gy")
    x, c = lev // 2, lev % 2
    partner = {"lev": 2 * x + 1 - c}
    next_row, last_row = {"gy": (g + 1) % 16}, {"gy": (g + 15) % 16}
    beside = {"lev": (lev + 1 + 6 * (1 - c)) % 8}
    barrier = pltpu.get_barrier_semaphore()
    for peer in [partner, beside, next_row, last_row] + [{"lev": (lev + 2 * d) % 8} for d in range(1, 4)]:
        pl.semaphore_signal(barrier, 1, device_id=peer, device_id_type=MESH)

    def copy(src, dst, at, peer):
        return pltpu.make_async_remote_copy(src_ref=src, dst_ref=dst, send_sem=ss.at[at], recv_sem=rs.at[at],
                                            device_id=peer, device_id_type=MESH)

    half = pl.ds(pl.multiple_of(48 * c, 48), 48)
    rest = pl.ds(pl.multiple_of(48 * (1 - c), 48), 48)
    weighted = fields_ref[3] * depth_ref[lev]
    own[...] = weighted.astype(BF)
    up_out[...] = fields_ref[2].astype(BF)
    edge_out[0] = fields_ref[1, 88:96]
    edge_out[1] = fields_ref[1, 0:8]
    pl.semaphore_wait(barrier, 7)
    all_rows = copy(own, other, 0, partner)
    some_rows = copy(own.at[0:48], other.at[0:48], 0, partner)

    @pl.when(c == 0)
    def _():
        all_rows.start()

    @pl.when(c == 1)
    def _():
        some_rows.start()

    winds = [copy(edge_out.at[0], edge_in.at[0], 1, next_row), copy(edge_out.at[1], edge_in.at[1], 2, last_row)]
    for w in winds:
        w.start()

    @pl.when(c == 0)
    def _():
        all_rows.wait_send()
        some_rows.wait_recv()

    @pl.when(c == 1)
    def _():
        some_rows.wait_send()
        all_rows.wait_recv()

    chip[...] = (own[half, :].astype(F32) + other[half, :].astype(F32)).astype(BF)
    sums = [copy(chip, lower.at[d - 1], 2 + d, {"lev": (lev + 2 * d) % 8}) for d in range(1, 4)]
    for d in range(1, 4):
        @pl.when(x + d <= 3)
        def _():
            sums[d - 1].start()

    rising = copy(up_out, up_in, 6, {"lev": (lev + 1) % 8})

    @pl.when(lev < 7)
    def _():
        rising.start()

    for w in winds:
        w.wait()
    east, north = fields_ref[0], fields_ref[1]
    out_ref[0] = diff_x(east) + diff_y(north, edge_in[0, 7:8], edge_in[1, 0:1]) + fields_ref[2]
    total[half, :] = jnp.zeros((48, NX), F32)
    for d in range(1, 4):
        @pl.when(x >= d)
        def _():
            sums[d - 1].wait_recv()
            total[half, :] += lower[d - 1].astype(F32)

    share[...] = total[half, :]
    shared = copy(share, total.at[half], 7, partner)
    shared.start()

    @pl.when(lev >= 1)
    def _():
        rising.wait_recv()
        out_ref[0] -= up_in[...].astype(F32)

    shared.wait()
    geo[...] = total[...] + fields_ref[3] * depth_ref[lev]

    @pl.when(c == 1)
    def _():
        geo[...] += other[...].astype(F32)

    edges = [copy(geo.at[88:96], edge_in.at[2], 8, next_row), copy(geo.at[0:8], edge_in.at[3], 9, last_row)]
    for e in edges:
        e.start()
    out_ref[1] = turning_ref[...] * north - diff_x(geo[...])
    for e in edges:
        e.wait()
    out_ref[2] = turning_ref[...] * east + diff_y(geo[...], edge_in[2, 7:8], edge_in[3, 0:1])
    for d in range(1, 4):
        @pl.when(x + d <= 3)
        def _():
            sums[d - 1].wait_send()

    @pl.when(lev < 7)
    def _():
        rising.wait_send()


def tail_step(fields, coriolis, layer_depth):
    vmem = pl.BlockSpec(memory_space=pltpu.VMEM)
    rows = (ROWS, NX)
    return pl.pallas_call(
        tail_body, name="tail_step", in_specs=[vmem, vmem, SMEM], out_specs=vmem,
        out_shape=jax.ShapeDtypeStruct((3, *rows), F32),
        scratch_shapes=[
            pltpu.VMEM(rows, BF), pltpu.VMEM(rows, BF), pltpu.VMEM((48, NX), BF), pltpu.VMEM((3, 48, NX), BF),
            pltpu.VMEM(rows, F32), pltpu.VMEM((48, NX), F32), pltpu.VMEM(rows, BF), pltpu.VMEM(rows, BF),
            pltpu.VMEM(rows, F32), pltpu.VMEM((2, 8, NX), F32), pltpu.VMEM((4, 8, NX), F32),
            pltpu.SemaphoreType.DMA((10,)), pltpu.SemaphoreType.DMA((10,)),
        ],
        compiler_params=pltpu.CompilerParams(collective_id=2, has_side_effects=True, vmem_limit_bytes=24 << 20),
    )(fields, coriolis[:, None], layer_depth)


@functools.lru_cache(None)
def kron_parts():
    order = np.arange(C).reshape(2, 8, 2).transpose(0, 2, 1).reshape(C)
    pick = np.zeros((C, C), np.float32)
    pick[np.arange(C), order] = 1.0
    spread = np.repeat(np.eye(C, dtype=np.float32), 16, 1)
    four = np.repeat(np.eye(4, dtype=np.float32), 16, 0)
    return [v.astype(BF) for v in (np.repeat(pick, 16, 0), spread, four, pick.T @ spread)]


def on_device(forcing, spectral_weight, point_weight, point_bias, decoder, coriolis, layer_depth):
    source = forcing[0]
    fwd, inv = (jnp.asarray(v) for v in x_tables())
    ytab = jnp.asarray(y_tables())
    pick, cols, four, dec_cols = [jnp.asarray(v) for v in kron_parts()]
    wt = point_weight.T
    state, back = steps(source, spectral_weight, ytab, fwd, inv, pick, wt, cols, point_bias)
    final, fields = last_local(back, state, source, pick, wt, cols, point_bias, four, decoder, dec_cols, inv)
    residual = tail_step(fields, coriolis, layer_depth)
    return final[None], residual[:, None]


def solution(mesh):
    return jax.shard_map(
        on_device,
        mesh=mesh,
        in_specs=(
            P("lev", None, "gy", None),
            P(None, "gy", None, None, None),
            P(),
            P(),
            P(),
            P("gy"),
            P(),
        ),
        out_specs=(P("lev", None, "gy", None), P(None, "lev", "gy", None)),
        check_vma=False,
    )
```

time: 205 us -> 159 us (0.78)
  Pallas kernels: 193 us -> 154 us
  local copies, waits for them, and re-layouts: 10.9 us -> 3.91 us
    pallas_call x8 -> x1, Pallas kernels: 159 us -> 120 us  [steps(): pl.pallas_call(steps_body, name='steps', in_specs=[any_space] * 5 + [vmem...]
    unnamed x28 -> x8, local copies, waits for them, and re-layouts: 10.8 us -> 3.8 us
where the time goes in v3:
time: 159 us
  Pallas kernels  154 us (97%)
  local copies, waits for them, and re-layouts  3.91 us (2%)
    pallas_call x1, Pallas kernels, steps(): pl.pallas_call(steps_body, name='steps', in_specs=[any_space] * 5 + [vmem...  120 us
    pallas_call x1, Pallas kernels, tail_step(): pl.pallas_call(tail_body, name='tail_step', in_specs=[vmem, vmem, SMEM],...  17.4 us
    pallas_call x1, Pallas kernels, last_local(): pl.pallas_call(last_body, name='last_local', grid=(ROWS // YC,), in_specs...  16.2 us
    unnamed x8, local copies, waits for them, and re-layouts  3.8 us

profile of v3, /device:TPU:2, one launch (start us, length us, event | category | flops | bytes accessed | tf_op | source)
XLA Modules:
  0.0 158.6 jit_solution(16065013149163643569)
XLA Ops:
  0.6 1.4 copy.16
  2.0 120.5 %steps.1 = (bf16[32,96,1024]{2,1,0:T(8,128)(2,1)}, bf16[2,4,96,1024]{3,2,1,0:T(8,128)(2,1)}) custom-call(bf16[32,96,1024]{2,1,0:T(8,128)(2,1)} %bitcast.8, bf16[2,8,32,32,128]{4,3,2,1,0:T(8,128)(2,1)} %weight_ref.1, bf16[2,4,384,256]{3,2,1,0:T(8,128)(2,1)} %constant.16.clone.ytab_ref, bf16[4,1024,256]{2,1,0:T(8,128)(2,1)} %constant.14.clone.fwd_hbm, ...), custom_call_target="tpu_custom_call" | custom-call | tf_op jit(solution)/shard_map/steps/pallas_call | solution.py:390
  122.5 0.0 copy-start.2
  122.5 0.0 copy-start.1
  122.5 16.2 %last_local.1 = (f32[32,96,1024]{2,1,0:T(8,128)}, f32[4,96,1024]{2,1,0:T(8,128)}) custom-call(bf16[2,4,96,1024]{3,2,1,0:T(8,128)(2,1)} %get-tuple-element.6.back_ref, bf16[32,96,1024]{2,1,0:T(8,128)(2,1)} %get-tuple-element.7.state_ref, bf16[32,96,1024]{2,1,0:T(8,128)(2,1)} %bitcast.9, bf16[512,32]{1,0:T(8,128)(2,1)} %constant.17.clone.pick_ref, ...), custom_call_target="tpu_custom_call" | custom-call | tf_op jit(solution)/shard_map/last_local/pallas_call | solution.py:132
  138.7 0.0 copy-done.2
  138.7 0.1 copy.17.turning_ref
  138.8 0.0 copy-done.1
  138.8 0.0 copy-start
  138.8 1.4 copy-done
  140.2 17.4 %tail_step.1 = f32[3,96,1024]{2,1,0:T(8,128)S(1)} custom-call(f32[4,96,1024]{2,1,0:T(8,128)S(1)} %copy-done, f32[96,1]{1,0:T(8,128)S(1)} %copy.17.turning_ref, f32[8]{0:T(128)S(1)} %copy-done.1), custom_call_target="tpu_custom_call" | custom-call | tf_op jit(solution)/shard_map/tail_step/pallas_call | solution.py:547
  157.6 1.0 copy.20
Async XLA Ops:
  122.5 16.2 %copy-start.2 = (f32[96]{0:T(128)S(1)}, f32[96]{0:T(128)}, u32[]{:S(2)}) copy-start(f32[96]{0:T(128)} %param.19) | copy-start | bytes 1156
  122.5 16.3 %copy-start.1 = (f32[8]{0:T(128)S(1)}, f32[8]{0:T(128)}, u32[]{:S(2)}) copy-start(f32[8]{0:T(128)} %depth_ref.1) | copy-start | bytes 100
  138.8 1.4 copy-start

commit v4 on v2

v4 whole, which is shorter than its diff:
```python
import functools
import math

import jax
import jax.numpy as jnp
import numpy as np
from jax import lax
from jax.experimental import pallas as pl
from jax.experimental.pallas import tpu as pltpu
from jax.sharding import PartitionSpec as P

C = 32
NX = 1024
NY = 1536
M = 128
ROWS = 96
ITERS = 3
MESH = pl.DeviceIdType.MESH
BF = jnp.bfloat16
F32 = jnp.float32
YC = 32
LC = 16
TILE = 256


def turns(a, b, length):
    phase = (a[:, None] * b[None, :]) % length
    return phase.astype(np.float32) * np.float32(2.0 * math.pi / length)


def lane_modes(half, order):
    p, r, s, j = np.meshgrid(np.array(order), np.arange(2), np.arange(4), np.arange(8), indexing="ij")
    k = 32 * s + 8 * p + j if half == 0 else 32 * p + 8 * s + j
    return k.reshape(-1), r.reshape(-1)


@functools.lru_cache(None)
def x_tables():
    forward, inverse = [], []
    for half in range(2):
        for order in ((0, 1, 2, 3), (1, 0, 3, 2)):
            k, r = lane_modes(half, order)
            turned = turns(np.arange(NX), k, NX)
            wave = np.where(r == 0, np.cos(turned), -np.sin(turned)).astype(np.float32)
            factor = np.where(k == 0, 1.0, 2.0).astype(np.float32) / np.float32(NX * NY)
            forward.append(wave)
            inverse.append((wave * factor[None, :]).T)
    return np.stack(forward).astype(BF), np.stack(inverse).astype(BF)


@functools.lru_cache(None)
def y_tables():
    m = np.arange(M)
    signed = np.where(m < M // 2, m, m + NY - M)
    rows = np.arange(NY)
    turned = turns(rows, signed, NY)
    both = np.concatenate([np.cos(turned), np.sin(turned)], 1).astype(np.float32).astype(BF)
    blocks = both.reshape(4, 4, ROWS, 2 * M)
    first = blocks.reshape(4, 4 * ROWS, 2 * M)
    second = blocks.transpose(1, 0, 2, 3).reshape(4, 4 * ROWS, 2 * M)
    return np.stack([first, second])


def gelu(v):
    inner = v * (math.sqrt(2.0 / math.pi) + (math.sqrt(2.0 / math.pi) * 0.044715) * (v * v))
    return (0.5 * v) * (1.0 + jnp.tanh(inner))


def lane_mask(rows):
    return lax.broadcasted_iota(jnp.int32, (rows, 128), 1) < 64


SMEM = pl.BlockSpec(memory_space=pltpu.SMEM)
LIMIT = 42 << 20


def shifted(field, step, axis):
    return pltpu.roll(field, step % field.shape[axis], axis)


def diff_x(field):
    return (shifted(field, -1, 1) - shifted(field, 1, 1)) * 0.5


def diff_y(field, before, after):
    at = lax.broadcasted_iota(jnp.int32, field.shape, 0)
    upper = jnp.where(at == field.shape[0] - 1, after, shifted(field, -1, 0))
    lower = jnp.where(at == 0, before, shifted(field, 1, 0))
    return (upper - lower) * 0.5


def tail_peers():
    lev = lax.axis_index("lev")
    g = lax.axis_index("gy")
    x, c = lev // 2, lev % 2
    beside = {"lev": (lev + 1 + 6 * (1 - c)) % 8}
    near_by = [{"lev": 2 * x + 1 - c}, beside, {"gy": (g + 1) % 16}, {"gy": (g + 15) % 16}]
    return near_by + [{"lev": (lev + 2 * d) % 8} for d in range(1, 4)]


def tail_body(fields_ref, turning_ref, depth_ref, out_ref, own, other, chip, lower, total, share, up_out, up_in,
              geo, edge_out, edge_in, ss, rs):
    lev = lax.axis_index("lev")
    g = lax.axis_index("gy")
    x, c = lev // 2, lev % 2
    partner = {"lev": 2 * x + 1 - c}
    next_row, last_row = {"gy": (g + 1) % 16}, {"gy": (g + 15) % 16}

    def copy(src, dst, at, peer):
        return pltpu.make_async_remote_copy(src_ref=src, dst_ref=dst, send_sem=ss.at[at], recv_sem=rs.at[at],
                                            device_id=peer, device_id_type=MESH)

    spot = lax.broadcasted_iota(jnp.int32, (ROWS, ROWS), 0) == lax.broadcasted_iota(jnp.int32, (ROWS, ROWS), 1)
    turning = jnp.sum(jnp.where(spot, jnp.broadcast_to(turning_ref[...], (ROWS, ROWS)), 0.0), 1, keepdims=True)
    half = pl.ds(pl.multiple_of(48 * c, 48), 48)
    rest = pl.ds(pl.multiple_of(48 * (1 - c), 48), 48)
    weighted = fields_ref[3] * depth_ref[lev]
    own[...] = weighted.astype(BF)
    up_out[...] = fields_ref[2].astype(BF)
    edge_out[0] = fields_ref[1, 88:96]
    edge_out[1] = fields_ref[1, 0:8]
    all_rows = copy(own, other, 0, partner)
    some_rows = copy(own.at[0:48], other.at[0:48], 0, partner)

    @pl.when(c == 0)
    def _():
        all_rows.start()

    @pl.when(c == 1)
    def _():
        some_rows.start()

    winds = [copy(edge_out.at[0], edge_in.at[0], 1, next_row), copy(edge_out.at[1], edge_in.at[1], 2, last_row)]
    for w in winds:
        w.start()

    @pl.when(c == 0)
    def _():
        all_rows.wait_send()
        some_rows.wait_recv()

    @pl.when(c == 1)
    def _():
        some_rows.wait_send()
        all_rows.wait_recv()

    chip[...] = (own[half, :].astype(F32) + other[half, :].astype(F32)).astype(BF)
    sums = [copy(chip, lower.at[d - 1], 2 + d, {"lev": (lev + 2 * d) % 8}) for d in range(1, 4)]
    for d in range(1, 4):
        @pl.when(x + d <= 3)
        def _():
            sums[d - 1].start()

    rising = copy(up_out, up_in, 6, {"lev": (lev + 1) % 8})

    @pl.when(lev < 7)
    def _():
        rising.start()

    for w in winds:
        w.wait()
    east, north = fields_ref[0], fields_ref[1]
    out_ref[0] = diff_x(east) + diff_y(north, edge_in[0, 7:8], edge_in[1, 0:1]) + fields_ref[2]
    total[half, :] = jnp.zeros((48, NX), F32)
    for d in range(1, 4):
        @pl.when(x >= d)
        def _():
            sums[d - 1].wait_recv()
            total[half, :] += lower[d - 1].astype(F32)

    share[...] = total[half, :]
    shared = copy(share, total.at[half], 7, partner)
    shared.start()

    @pl.when(lev >= 1)
    def _():
        rising.wait_recv()
        out_ref[0] -= up_in[...].astype(F32)

    shared.wait()
    geo[...] = total[...] + fields_ref[3] * depth_ref[lev]

    @pl.when(c == 1)
    def _():
        geo[...] += other[...].astype(F32)

    edges = [copy(geo.at[88:96], edge_in.at[2], 8, next_row), copy(geo.at[0:8], edge_in.at[3], 9, last_row)]
    for e in edges:
        e.start()
    out_ref[1] = turning * north - diff_x(geo[...])
    for e in edges:
        e.wait()
    out_ref[2] = turning * east + diff_y(geo[...], edge_in[2, 7:8], edge_in[3, 0:1])
    for d in range(1, 4):
        @pl.when(x + d <= 3)
        def _():
            sums[d - 1].wait_send()

    @pl.when(lev < 7)
    def _():
        rising.wait_send()


def dot_last(left, right):
    return lax.dot_general(left, right, (((1,), (1,)), ((), ())), preferred_element_type=F32)


def kron_values(left, cols):
    left = left.astype(BF)
    full = jnp.dot(left, cols, preferred_element_type=F32)
    i = lax.broadcasted_iota(jnp.int32, full.shape, 0) % 16
    j = lax.broadcasted_iota(jnp.int32, full.shape, 1) % 16
    return jnp.where(i == j, full, 0.0).astype(BF)


def steps_body(forcing_ref, weight_ref, ytab_ref, fwd_hbm, inv_hbm, pick_ref, wt_ref, cols_ref, four_ref, dec_ref,
               dcols_ref, turning_ref, bias_ref, depth_ref, final, out_ref,
               source, state, fwd, inv, kron, wbuf, tabs, near, r1, part, s2, r2, sp, mx, acc, r3, m2, s4, back,
               dmat, hold, fields, own_heat, other_heat, chip, lower, total, share, up_out, up_in, geo,
               edge_out, edge_in, ts, tr, lsem, s1s, s1r, s2s, s2r, s3s, s3r, s4s, s4r):
    g = lax.axis_index("gy")
    z, y = g // 4, g % 4
    own = ((y, z), (z, y))

    def first_peer(h, a):
        return {"gy": z * 4 + a} if h == 0 else {"gy": a * 4 + y}

    def second_peer(h, b):
        return {"gy": b * 4 + y} if h == 0 else {"gy": z * 4 + b}

    barrier = pltpu.get_barrier_semaphore()
    for h in range(2):
        for d in range(1, 4):
            pl.semaphore_signal(barrier, 1, device_id=first_peer(h, (own[h][0] + d) % 4), device_id_type=MESH)

    for peer in tail_peers():
        pl.semaphore_signal(barrier, 1, device_id=peer, device_id_type=MESH)

    def rows_of(k):
        return pl.ds(pl.multiple_of(k * YC, YC), YC)

    def few_of(k):
        return pl.ds(pl.multiple_of(k * LC, LC), LC)

    chunks = ROWS // YC
    pieces = ROWS // LC
    early = 64 // LC

    def local(src, dst, at):
        return pltpu.make_async_copy(src, dst, lsem.at[at])

    load_fwd = local(fwd_hbm, fwd, 0)
    load_source = [local(forcing_ref.at[:, rows_of(k)], source.at[:, rows_of(k)], 1 + k) for k in range(chunks)]
    load_tabs = [local(ytab_ref.at[h, own[h][1]], tabs.at[h], 4 + h) for h in range(2)]
    load_weights = local(weight_ref, wbuf, 6)
    load_inv = local(inv_hbm, inv, 7)
    load_state = local(forcing_ref, state, 8)
    for c in [load_fwd, *load_source, *load_tabs, load_weights, load_inv, load_state]:
        c.start()

    def remote(src, dst, send, recv, peer):
        return pltpu.make_async_remote_copy(src_ref=src, dst_ref=dst, send_sem=send, recv_sem=recv, device_id=peer,
                                            device_id_type=MESH)

    def one(h, d, k):
        a = own[h][0]
        return remote(near.at[h, (a + d) % 4, few_of(k)], r1.at[h, a, few_of(k)], s1s.at[h, d - 1, k],
                      s1r.at[h, d - 1, k], first_peer(h, (a + d) % 4))

    def two(h, d):
        b = own[h][1]
        return remote(s2.at[h, (b + d) % 4], r2.at[h, d - 1], s2s.at[h, d - 1], s2r.at[h, d - 1],
                      second_peer(h, (b + d) % 4))

    def three(h, d):
        b = own[h][1]
        return remote(r3.at[h, b], r3.at[h, b], s3s.at[h, d - 1], s3r.at[h, d - 1], second_peer(h, (b + d) % 4))

    def four(h, d, k):
        a = own[h][0]
        return remote(s4.at[h, (a + d) % 4, rows_of(k)], back.at[h, a, rows_of(k)], s4s.at[h, d - 1, k],
                      s4r.at[h, d - 1, k], first_peer(h, (a + d) % 4))

    def forward(k, load):
        rows = few_of(k)
        mask = lane_mask(LC)
        for h in range(2):
            outs = []
            for par in range(2):
                lhs = jnp.concatenate([load(16 * h + 2 * pair + par, rows) for pair in range(8)], 0)
                outs.append(jnp.dot(lhs, fwd[2 * h + par], preferred_element_type=F32))
            even, odd = outs
            for pair in range(8):
                at = slice(pair * LC, (pair + 1) * LC)
                for v in range(2):
                    e = even[at, 128 * v:128 * v + 128]
                    o = odd[at, 128 * v:128 * v + 128]
                    lanes = slice(128 * pair, 128 * pair + 128)
                    near[h, 2 * v, rows, lanes] = jnp.where(mask, e, o).astype(BF)
                    near[h, 2 * v + 1, rows, lanes] = jnp.where(mask, o, e).astype(BF)
            for d in range(1, 4):
                one(h, d, k).start()
            a = own[h][0]
            r1[h, a, rows] = near[h, a, rows]

    def update(k, sink):
        rows = few_of(k)
        mask = lane_mask(LC)
        groups = []
        for h in range(2):
            even, odd = [], []
            for pair in range(8):
                b = [back[h, p, rows, 128 * pair:128 * pair + 128] for p in range(4)]
                even.append(jnp.concatenate([jnp.where(mask, b[0], b[1]), jnp.where(mask, b[2], b[3])], 1))
                odd.append(jnp.concatenate([jnp.where(mask, b[1], b[0]), jnp.where(mask, b[3], b[2])], 1))
            groups.append(jnp.concatenate(even, 0))
            groups.append(jnp.concatenate(odd, 0))
        for t in range(NX // TILE):
            cols = slice(t * TILE, (t + 1) * TILE)
            mixed = []
            for s in range(LC // 16):
                at = pl.ds(pl.multiple_of(k * LC + 16 * s, 16), 16)
                st = state[:, at, cols].reshape(C * 16, TILE)
                mixed.append(jnp.dot(kron[...], st, preferred_element_type=F32).reshape(4, 8, 16, TILE))
            for q in range(4):
                h, par = q // 2, q % 2
                spread = jnp.dot(groups[q], inv[q, :, cols], preferred_element_type=F32)
                spread = spread.reshape(8, LC, TILE)
                for pair in range(8):
                    c = 16 * h + 2 * pair + par
                    pw = jnp.concatenate([m[q, pair] for m in mixed], 0)
                    v = spread[pair] + pw + (source[c, rows, cols].astype(F32) + bias_ref[c])
                    sink(q, pair, c, rows, cols, gelu(v))

    def keep_state(q, pair, c, rows, cols, value):
        state[c, rows, cols] = value.astype(BF)

    def keep_final(q, pair, c, rows, cols, value):
        final[c, rows, cols] = value
        hold[8 * q + pair, :, cols] = value.astype(BF)

    pl.semaphore_wait(barrier, 13)
    load_fwd.wait()

    @pl.loop(0, chunks)
    def _(k):
        pltpu.make_async_copy(forcing_ref.at[:, rows_of(k)], source.at[:, rows_of(k)], lsem.at[1 + k]).wait()
        pl.loop(0, YC // LC)(lambda t: forward(k * (YC // LC) + t, lambda c, rows: source[c, rows]))

    kron[...] = kron_values(dot_last(pick_ref[...], wt_ref[...]), cols_ref[...])
    dmat[...] = kron_values(jnp.dot(four_ref[...], dec_ref[...], preferred_element_type=F32), dcols_ref[...])
    for c in [*load_tabs, load_weights, load_inv, load_state]:
        c.wait()

    @pl.loop(0, ITERS)
    def _(it):
        for h in range(2):
            for k in range(early):
                for d in range(1, 4):
                    one(h, d, k).wait()

            @pl.loop(0, 4)
            def _(n):
                cols = pl.ds(pl.multiple_of(n * 256, 256), 256)
                x = r1[h, :, 0:64, cols].reshape(256, 256)
                table = tabs[h].reshape(4, ROWS, 2 * M)[:, 0:64].reshape(256, 2 * M)
                acc[h, n] = lax.dot_general(x, table, (((0,), (0,)), ((), ())), preferred_element_type=F32)

        for h in range(2):
            a, b = own[h]
            for k in range(early, pieces):
                for d in range(1, 4):
                    one(h, d, k).wait()

            @pl.loop(0, 4)
            def _(n):
                cols = pl.ds(pl.multiple_of(n * 256, 256), 256)
                x = r1[h, :, 64:96, cols].reshape(128, 256)
                table = tabs[h].reshape(4, ROWS, 2 * M)[:, 64:96].reshape(128, 2 * M)
                pt = acc[h, n] + lax.dot_general(x, table, (((0,), (0,)), ((), ())), preferred_element_type=F32)
                pt = pt.reshape(2, 2, 2, 4, 8, 256)
                for pair in range(2):
                    for h2 in range(2):
                        q0, q1 = pt[pair, h2, 0], pt[pair, h2, 1]
                        re = q0[..., :M] + q1[..., M:]
                        im = q1[..., :M] - q0[..., M:]
                        both = jnp.concatenate([re, im], 1)
                        c = 2 * (2 * n + pair) + lax.rem(h2 + a, 2)
                        part[h, :, c] = both
                        s2[h, :, c] = both.astype(BF)

            for d in range(1, 4):
                two(h, d).start()
        for h in range(2):
            b = own[h][1]
            for d in range(1, 4):
                two(h, d).wait()

            @pl.loop(0, 16)
            def _(c):
                total = part[h, b, c]
                for d in range(3):
                    total = total + r2[h, d, c].astype(F32)
                sp[16 * h + c] = total

            for oh in range(2):
                outs = pl.ds(16 * oh, 16)
                for j in range(8):
                    def add(i, acc):
                        ar, ai = acc
                        wr = wbuf[0, j, i, outs].astype(F32)
                        wi = wbuf[1, j, i, outs].astype(F32)
                        sr = jnp.broadcast_to(sp[i, pl.ds(j, 1), :], (16, M))
                        si = jnp.broadcast_to(sp[i, pl.ds(8 + j, 1), :], (16, M))
                        return ar + (sr * wr - si * wi), ai + (sr * wi + si * wr)

                    re_at, im_at = pl.ds(j, 16, stride=16), pl.ds(8 + j, 16, stride=16)
                    if h == 0:
                        begin = (jnp.zeros((16, M), F32), jnp.zeros((16, M), F32))
                    else:
                        begin = (mx[oh, re_at, :], mx[oh, im_at, :])
                    ar, ai = lax.fori_loop(16 * h, 16 * h + 16, add, begin, unroll=8)
                    mx[oh, re_at, :] = ar
                    mx[oh, im_at, :] = ai
                if h == 1:
                    r3[oh, own[oh][1]] = mx[oh].reshape(16, 16, M).astype(BF)
                    for d in range(1, 4):
                        three(oh, d).start()

        def back_chunk(h, k):
            rows = rows_of(k)
            a = own[h][0]
            left = jnp.concatenate([tabs[h, pl.ds(pl.multiple_of(ROWS * p + k * YC, YC), YC)] for p in range(4)], 0)
            for n in range(4):
                lanes = slice(256 * n, 256 * n + 256)
                out = lax.dot_general(left, m2[h, lanes], (((1,), (1,)), ((), ())), preferred_element_type=F32)
                s4[h, :, rows, lanes] = out.reshape(4, YC, 256).astype(BF)
            for d in range(1, 4):
                four(h, d, k).start()
            back[h, a, rows] = s4[h, a, rows]

        for h in range(2):
            a = own[h][0]
            for d in range(1, 4):
                three(h, d).wait()

            @pl.loop(0, 8)
            def _(n):
                rows = []
                for h2 in range(2):
                    c = 2 * n + lax.rem(h2 + a, 2)
                    block = r3[h, :, c].astype(F32).reshape(4, 2, 8, M)
                    re = block[:, 0].reshape(32, M)
                    im = block[:, 1].reshape(32, M)
                    rows.append(jnp.concatenate([re, -im], 1))
                    rows.append(jnp.concatenate([im, re], 1))
                m2[h, pl.ds(pl.multiple_of(n * 128, 128), 128)] = jnp.concatenate(rows, 0).astype(BF)

            back_chunk(h, 0)

        @pl.loop(1, chunks)
        def _(k):
            for h in range(2):
                back_chunk(h, k)

        @pl.when(it < ITERS - 1)
        def _():
            @pl.loop(0, chunks)
            def _(k):
                for h in range(2):
                    for d in range(1, 4):
                        four(h, d, k).wait()

                @pl.loop(0, YC // LC)
                def _(t):
                    update(k * (YC // LC) + t, keep_state)
                    forward(k * (YC // LC) + t, lambda c, rows: state[c, rows])

    @pl.loop(0, chunks)
    def _(k):
        for h in range(2):
            for d in range(1, 4):
                four(h, d, k).wait()

        @pl.loop(0, YC // LC)
        def _(t):
            piece = k * (YC // LC) + t
            rows = few_of(piece)
            update(piece, keep_final)
            for s in range(LC // 16):
                part_rows = pl.ds(pl.multiple_of(piece * LC + 16 * s, 16), 16)
                lhs = hold[:, 16 * s:16 * s + 16, :].reshape(C * 16, NX)
                f = jnp.dot(dmat[...], lhs, preferred_element_type=F32)
                fields[:, part_rows, :] = f.reshape(4, 16, NX)

    tail_body(fields, turning_ref, depth_ref, out_ref, own_heat, other_heat, chip, lower, total, share, up_out, up_in,
              geo, edge_out, edge_in, ts, tr)


def steps(forcing, weights, ytab, fwd, inv, pick, wt, cols, four, dec, dcols, turning, bias, depth):
    near_shape = (2, 4, ROWS, NX)
    chunks = ROWS // YC
    flat = (ROWS, NX)
    any_space = pl.BlockSpec(memory_space=pl.ANY)
    vmem = pl.BlockSpec(memory_space=pltpu.VMEM)
    dma = pltpu.SemaphoreType.DMA
    return pl.pallas_call(
        steps_body, name="steps",
        in_specs=[any_space] * 5 + [vmem] * 7 + [SMEM] * 2,
        out_specs=[vmem, vmem],
        out_shape=[pltpu.VMEM((C, ROWS, NX), F32), pltpu.VMEM((3, ROWS, NX), F32)],
        scratch_shapes=[
            pltpu.VMEM((C, ROWS, NX), BF),
            pltpu.VMEM((C, ROWS, NX), BF),
            pltpu.VMEM(fwd.shape, BF),
            pltpu.VMEM(inv.shape, BF),
            pltpu.VMEM((C * 16, C * 16), BF),
            pltpu.VMEM((2, 8, C, C, M), BF),
            pltpu.VMEM((2, 4 * ROWS, 2 * M), BF),
            pltpu.VMEM(near_shape, BF),
            pltpu.VMEM(near_shape, BF),
            pltpu.VMEM((2, 4, 16, 16, M), F32),
            pltpu.VMEM((2, 4, 16, 16, M), BF),
            pltpu.VMEM((2, 3, 16, 16, M), BF),
            pltpu.VMEM((C, 16, M), F32),
            pltpu.VMEM((2, 16 * 16, M), F32),
            pltpu.VMEM((2, 4, 256, 256), F32),
            pltpu.VMEM((2, 4, 16, 16, M), BF),
            pltpu.VMEM((2, NX, 2 * M), BF),
            pltpu.VMEM(near_shape, BF),
            pltpu.VMEM(near_shape, BF),
            pltpu.VMEM((64, C * 16), BF), pltpu.VMEM((C, LC, NX), BF),
            pltpu.VMEM((4, ROWS, NX), F32),
            pltpu.VMEM(flat, BF), pltpu.VMEM(flat, BF), pltpu.VMEM((48, NX), BF), pltpu.VMEM((3, 48, NX), BF),
            pltpu.VMEM(flat, F32), pltpu.VMEM((48, NX), F32), pltpu.VMEM(flat, BF), pltpu.VMEM(flat, BF),
            pltpu.VMEM(flat, F32), pltpu.VMEM((2, 8, NX), F32), pltpu.VMEM((4, 8, NX), F32), dma((10,)), dma((10,)),
            dma((9,)),
            dma((2, 3, ROWS // LC)), dma((2, 3, ROWS // LC)),
            dma((2, 3)), dma((2, 3)), dma((2, 3)), dma((2, 3)),
            dma((2, 3, chunks)), dma((2, 3, chunks)),
        ],
        compiler_params=pltpu.CompilerParams(collective_id=1, has_side_effects=True, vmem_limit_bytes=LIMIT),
    )(forcing, weights, ytab, fwd, inv, pick, wt, cols, four, dec, dcols, turning, bias, depth)


def finish_body(final_ref, residual_ref, final_out, residual_out, sem):
    copies = [pltpu.make_async_copy(final_ref.at[pl.ds(4 * i, 4)], final_out.at[pl.ds(4 * i, 4)], sem.at[i]) for i in range(8)]
    copies.append(pltpu.make_async_copy(residual_ref, residual_out, sem.at[8]))
    for c in copies:
        c.start()
    for c in copies:
        c.wait()


def finish(final, residual):
    any_space = pl.BlockSpec(memory_space=pl.ANY)
    return pl.pallas_call(
        finish_body, name="finish", in_specs=[pl.BlockSpec(memory_space=pltpu.VMEM)] * 2, out_specs=[any_space] * 2,
        out_shape=[jax.ShapeDtypeStruct(final.shape, F32), jax.ShapeDtypeStruct(residual.shape, F32)],
        scratch_shapes=[pltpu.SemaphoreType.DMA((9,))],
        compiler_params=pltpu.CompilerParams(vmem_limit_bytes=1 << 20),
    )(final, residual)


@functools.lru_cache(None)
def kron_parts():
    order = np.arange(C).reshape(2, 8, 2).transpose(0, 2, 1).reshape(C)
    pick = np.zeros((C, C), np.float32)
    pick[np.arange(C), order] = 1.0
    spread = np.repeat(np.eye(C, dtype=np.float32), 16, 1)
    four = np.repeat(np.eye(4, dtype=np.float32), 16, 0)
    return [v.astype(BF) for v in (np.repeat(pick, 16, 0), spread, four, pick.T @ spread)]


def on_device(forcing, spectral_weight, point_weight, point_bias, decoder, coriolis, layer_depth):
    source = forcing[0]
    fwd, inv = (jnp.asarray(v) for v in x_tables())
    ytab = jnp.asarray(y_tables())
    pick, cols, four, dec_cols = [jnp.asarray(v) for v in kron_parts()]
    final, residual = steps(source, spectral_weight, ytab, fwd, inv, pick, point_weight, cols, four, decoder, dec_cols,
                            coriolis[None], point_bias, layer_depth)
    final, residual = finish(final, residual)
    return final[None], residual[:, None]


def solution(mesh):
    return jax.shard_map(
        on_device,
        mesh=mesh,
        in_specs=(
            P("lev", None, "gy", None),
            P(None, "gy", None, None, None),
            P(),
            P(),
            P(),
            P("gy"),
            P(),
        ),
        out_specs=(P("lev", None, "gy", None), P(None, "lev", "gy", None)),
        check_vma=False,
    )
```

time: 205 us -> 140 us (0.68)
  Pallas kernels: 193 us -> 139 us
  local copies, waits for them, and re-layouts: 10.9 us -> 0 us
    pallas_call x10 -> x2, Pallas kernels: 193 us -> 139 us  [the longest x1 134 us: steps(): pl.pallas_call(steps_body, name='steps', in_specs=[any_space] * 5 + [vmem...]
    unnamed x28 -> x0, local copies, waits for them, and re-layouts: 10.8 us -> none
where the time goes in v4:
time: 140 us; the launch traced here: 139 us
  Pallas kernels  139 us (99%)
    pallas_call x1, Pallas kernels, steps(): pl.pallas_call(steps_body, name='steps', in_specs=[any_space] * 5 + [vmem...  134 us
    pallas_call x1, Pallas kernels, finish(): pl.pallas_call(finish_body, name='finish', in_specs=[pl.BlockSpec(memory_...  5.01 us

profile of v4, /device:TPU:2, one launch (start us, length us, event | category | flops | bytes accessed | tf_op | source)
XLA Modules:
  0.0 139.4 jit_solution(8594690745031254278)
XLA Ops:
  0.6 133.7 %steps.1 = (f32[32,96,1024]{2,1,0:T(8,128)S(1)}, f32[3,96,1024]{2,1,0:T(8,128)S(1)}) custom-call(bf16[32,96,1024]{2,1,0:T(8,128)(2,1)} %bitcast.6, bf16[2,8,32,32,128]{4,3,2,1,0:T(8,128)(2,1)} %weight_ref.1, bf16[2,4,384,256]{3,2,1,0:T(8,128)(2,1)} %constant.16.clone.ytab_ref, bf16[4,1024,256]{2,1,0:T(8,128)(2,1)} %constant.14.clone.fwd_hbm, ...), custom_call_target="tpu_custom_call" | custom-call | tf_op jit(solution)/shard_map/steps/pallas_call | solution.py:507
  134.4 5.0 %finish.1 = (f32[32,96,1024]{2,1,0:T(8,128)}, f32[3,96,1024]{2,1,0:T(8,128)}) custom-call(f32[32,96,1024]{2,1,0:T(8,128)S(1)} %get-tuple-element.6.final_ref, f32[3,96,1024]{2,1,0:T(8,128)S(1)} %get-tuple-element.7.residual_ref), custom_call_target="tpu_custom_call" | custom-call | tf_op jit(solution)/shard_map/finish/pallas_call | solution.py:557

commit v5 on v4

--- a/solution.py
+++ b/solution.py
@@ -19,7 +19,8 @@
 BF = jnp.bfloat16
 F32 = jnp.float32
 YC = 32
-LC = 16
+LC = 32
+SPLIT = 3
 TILE = 256
 
 
@@ -317,20 +318,26 @@
             groups.append(jnp.concatenate(odd, 0))
         for t in range(NX // TILE):
             cols = slice(t * TILE, (t + 1) * TILE)
-            mixed = []
-            for s in range(LC // 16):
-                at = pl.ds(pl.multiple_of(k * LC + 16 * s, 16), 16)
-                st = state[:, at, cols].reshape(C * 16, TILE)
-                mixed.append(jnp.dot(kron[...], st, preferred_element_type=F32).reshape(4, 8, 16, TILE))
             for q in range(4):
                 h, par = q // 2, q % 2
                 spread = jnp.dot(groups[q], inv[q, :, cols], preferred_element_type=F32)
                 spread = spread.reshape(8, LC, TILE)
                 for pair in range(8):
                     c = 16 * h + 2 * pair + par
-                    pw = jnp.concatenate([m[q, pair] for m in mixed], 0)
-                    v = spread[pair] + pw + (source[c, rows, cols].astype(F32) + bias_ref[c])
-                    sink(q, pair, c, rows, cols, gelu(v))
+                    sink(q, pair, c, rows, cols, gelu(final[c, rows, cols] + spread[pair]))
+
+    def prepare(first, last):
+        @pl.loop(first, last)
+        def _(k):
+            rows = pl.ds(pl.multiple_of(16 * k, 16), 16)
+            for t in range(NX // TILE):
+                cols = slice(t * TILE, (t + 1) * TILE)
+                st = state[:, rows, cols].reshape(C * 16, TILE)
+                mixed = jnp.dot(kron[...], st, preferred_element_type=F32).reshape(4, 8, 16, TILE)
+                for q in range(4):
+                    for pair in range(8):
+                        c = 16 * (q // 2) + 2 * pair + q % 2
+                        final[c, rows, cols] = mixed[q, pair] + (source[c, rows, cols].astype(F32) + bias_ref[c])
 
     def keep_state(q, pair, c, rows, cols, value):
         state[c, rows, cols] = value.astype(BF)
@@ -391,6 +398,8 @@
 
             for d in range(1, 4):
                 two(h, d).start()
+
+        prepare(0, SPLIT)
         for h in range(2):
             b = own[h][1]
             for d in range(1, 4):
@@ -426,6 +435,8 @@
                     r3[oh, own[oh][1]] = mx[oh].reshape(16, 16, M).astype(BF)
                     for d in range(1, 4):
                         three(oh, d).start()
+
+        prepare(SPLIT, 6)
 
         def back_chunk(h, k):
             rows = rows_of(k)

time: 140 us -> 130 us (0.929)
  Pallas kernels: 139 us -> 128 us
    pallas_call x1, Pallas kernels: 134 us -> 123 us  [steps(): pl.pallas_call(steps_body, name='steps', in_specs=[any_space] * 5 + [vmem...]
where the time goes in v5:
time: 130 us; the launch traced here: 129 us
  Pallas kernels  128 us (98%)
    pallas_call x1, Pallas kernels, steps(): pl.pallas_call(steps_body, name='steps', in_specs=[any_space] * 5 + [vmem...  123 us
    pallas_call x1, Pallas kernels, finish(): pl.pallas_call(finish_body, name='finish', in_specs=[pl.BlockSpec(memory_...  5.01 us

profile of v5, /device:TPU:2, one launch (start us, length us, event | category | flops | bytes accessed | tf_op | source)
XLA Modules:
  0.0 128.9 jit_solution(12693272959068942601)
XLA Ops:
  0.6 123.2 %steps.1 = (f32[32,96,1024]{2,1,0:T(8,128)S(1)}, f32[3,96,1024]{2,1,0:T(8,128)S(1)}) custom-call(bf16[32,96,1024]{2,1,0:T(8,128)(2,1)} %bitcast.6, bf16[2,8,32,32,128]{4,3,2,1,0:T(8,128)(2,1)} %weight_ref.1, bf16[2,4,384,256]{3,2,1,0:T(8,128)(2,1)} %constant.16.clone.ytab_ref, bf16[4,1024,256]{2,1,0:T(8,128)(2,1)} %constant.14.clone.fwd_hbm, ...), custom_call_target="tpu_custom_call" | custom-call | tf_op jit(solution)/shard_map/steps/pallas_call | solution.py:518
  123.9 5.0 %finish.1 = (f32[32,96,1024]{2,1,0:T(8,128)}, f32[3,96,1024]{2,1,0:T(8,128)}) custom-call(f32[32,96,1024]{2,1,0:T(8,128)S(1)} %get-tuple-element.6.final_ref, f32[3,96,1024]{2,1,0:T(8,128)S(1)} %get-tuple-element.7.residual_ref), custom_call_target="tpu_custom_call" | custom-call | tf_op jit(solution)/shard_map/finish/pallas_call | solution.py:568

commit v6 on v5

--- a/solution.py
+++ b/solution.py
@@ -215,9 +215,9 @@
 
 
 def steps_body(forcing_ref, weight_ref, ytab_ref, fwd_hbm, inv_hbm, pick_ref, wt_ref, cols_ref, four_ref, dec_ref,
-               dcols_ref, turning_ref, bias_ref, depth_ref, final, out_ref,
-               source, state, fwd, inv, kron, wbuf, tabs, near, r1, part, s2, r2, sp, mx, acc, r3, m2, s4, back,
-               dmat, hold, fields, own_heat, other_heat, chip, lower, total, share, up_out, up_in, geo,
+               turning_ref, bias_ref, depth_ref, final, out_ref,
+               source, state, fwd, inv, kron, wbuf, tabs, near, r1, part, s2, r2, sp, mx, r3, m2, s4, back,
+               dmat, fields, own_heat, other_heat, chip, lower, total, share, up_out, up_in, geo,
                edge_out, edge_in, ts, tr, lsem, s1s, s1r, s2s, s2r, s3s, s3r, s4s, s4r):
     g = lax.axis_index("gy")
     z, y = g // 4, g % 4
@@ -245,7 +245,6 @@
 
     chunks = ROWS // YC
     pieces = ROWS // LC
-    early = 64 // LC
 
     def local(src, dst, at):
         return pltpu.make_async_copy(src, dst, lsem.at[at])
@@ -263,54 +262,60 @@
         return pltpu.make_async_remote_copy(src_ref=src, dst_ref=dst, send_sem=send, recv_sem=recv, device_id=peer,
                                             device_id_type=MESH)
 
-    def one(h, d, k):
+    def lanes_of(e):
+        return slice(512 * e, 512 * e + 512)
+
+    def one(h, d, k, e):
         a = own[h][0]
-        return remote(near.at[h, (a + d) % 4, few_of(k)], r1.at[h, a, few_of(k)], s1s.at[h, d - 1, k],
-                      s1r.at[h, d - 1, k], first_peer(h, (a + d) % 4))
-
-    def two(h, d):
+        return remote(near.at[h, (a + d) % 4, few_of(k), lanes_of(e)], r1.at[h, a, few_of(k), lanes_of(e)],
+                      s1s.at[e, h, d - 1, k], s1r.at[e, h, d - 1, k], first_peer(h, (a + d) % 4))
+
+    def two(h, d, e):
         b = own[h][1]
-        return remote(s2.at[h, (b + d) % 4], r2.at[h, d - 1], s2s.at[h, d - 1], s2r.at[h, d - 1],
+        at = pl.ds(8 * e, 8)
+        return remote(s2.at[h, (b + d) % 4, at], r2.at[h, d - 1, at], s2s.at[e, h, d - 1], s2r.at[e, h, d - 1],
                       second_peer(h, (b + d) % 4))
 
-    def three(h, d):
+    def three(h, d, e):
         b = own[h][1]
-        return remote(r3.at[h, b], r3.at[h, b], s3s.at[h, d - 1], s3r.at[h, d - 1], second_peer(h, (b + d) % 4))
-
-    def four(h, d, k):
+        at = pl.ds(8 * e, 8)
+        return remote(r3.at[h, b, at], r3.at[h, b, at], s3s.at[e, h, d - 1], s3r.at[e, h, d - 1],
+                      second_peer(h, (b + d) % 4))
+
+    def four(h, d, k, e):
         a = own[h][0]
-        return remote(s4.at[h, (a + d) % 4, rows_of(k)], back.at[h, a, rows_of(k)], s4s.at[h, d - 1, k],
-                      s4r.at[h, d - 1, k], first_peer(h, (a + d) % 4))
-
-    def forward(k, load):
+        return remote(s4.at[h, (a + d) % 4, rows_of(k), lanes_of(e)], back.at[h, a, rows_of(k), lanes_of(e)],
+                      s4s.at[e, h, d - 1, k], s4r.at[e, h, d - 1, k], first_peer(h, (a + d) % 4))
+
+    def forward(k, load, e):
         rows = few_of(k)
         mask = lane_mask(LC)
         for h in range(2):
             outs = []
             for par in range(2):
-                lhs = jnp.concatenate([load(16 * h + 2 * pair + par, rows) for pair in range(8)], 0)
+                lhs = jnp.concatenate([load(16 * h + 2 * pair + par, rows) for pair in range(4 * e, 4 * e + 4)], 0)
                 outs.append(jnp.dot(lhs, fwd[2 * h + par], preferred_element_type=F32))
             even, odd = outs
-            for pair in range(8):
-                at = slice(pair * LC, (pair + 1) * LC)
+            for pair in range(4 * e, 4 * e + 4):
+                at = slice((pair - 4 * e) * LC, (pair - 4 * e + 1) * LC)
                 for v in range(2):
-                    e = even[at, 128 * v:128 * v + 128]
-                    o = odd[at, 128 * v:128 * v + 128]
+                    lo = even[at, 128 * v:128 * v + 128]
+                    hi = odd[at, 128 * v:128 * v + 128]
                     lanes = slice(128 * pair, 128 * pair + 128)
-                    near[h, 2 * v, rows, lanes] = jnp.where(mask, e, o).astype(BF)
-                    near[h, 2 * v + 1, rows, lanes] = jnp.where(mask, o, e).astype(BF)
+                    near[h, 2 * v, rows, lanes] = jnp.where(mask, lo, hi).astype(BF)
+                    near[h, 2 * v + 1, rows, lanes] = jnp.where(mask, hi, lo).astype(BF)
             for d in range(1, 4):
-                one(h, d, k).start()
+                one(h, d, k, e).start()
             a = own[h][0]
-            r1[h, a, rows] = near[h, a, rows]
-
-    def update(k, sink):
+            r1[h, a, rows, lanes_of(e)] = near[h, a, rows, lanes_of(e)]
+
+    def update(k, sink, e):
         rows = few_of(k)
         mask = lane_mask(LC)
         groups = []
         for h in range(2):
             even, odd = [], []
-            for pair in range(8):
+            for pair in range(4 * e, 4 * e + 4):
                 b = [back[h, p, rows, 128 * pair:128 * pair + 128] for p in range(4)]
                 even.append(jnp.concatenate([jnp.where(mask, b[0], b[1]), jnp.where(mask, b[2], b[3])], 1))
                 odd.append(jnp.concatenate([jnp.where(mask, b[1], b[0]), jnp.where(mask, b[3], b[2])], 1))
@@ -321,10 +326,10 @@
             for q in range(4):
                 h, par = q // 2, q % 2
                 spread = jnp.dot(groups[q], inv[q, :, cols], preferred_element_type=F32)
-                spread = spread.reshape(8, LC, TILE)
-                for pair in range(8):
+                spread = spread.reshape(4, LC, TILE)
+                for pair in range(4 * e, 4 * e + 4):
                     c = 16 * h + 2 * pair + par
-                    sink(q, pair, c, rows, cols, gelu(final[c, rows, cols] + spread[pair]))
+                    sink(q, pair, c, rows, cols, gelu(final[c, rows, cols] + spread[pair - 4 * e]))
 
     def prepare(first, last):
         @pl.loop(first, last)
@@ -344,7 +349,7 @@
 
     def keep_final(q, pair, c, rows, cols, value):
         final[c, rows, cols] = value
-        hold[8 * q + pair, :, cols] = value.astype(BF)
+        state[c, rows, cols] = value.astype(BF)
 
     pl.semaphore_wait(barrier, 13)
     load_fwd.wait()
@@ -352,60 +357,48 @@
     @pl.loop(0, chunks)
     def _(k):
         pltpu.make_async_copy(forcing_ref.at[:, rows_of(k)], source.at[:, rows_of(k)], lsem.at[1 + k]).wait()
-        pl.loop(0, YC // LC)(lambda t: forward(k * (YC // LC) + t, lambda c, rows: source[c, rows]))
+        pl.loop(0, YC // LC)(lambda t: [forward(k * (YC // LC) + t, lambda c, rows: source[c, rows], e) for e in range(2)] and None)
 
     kron[...] = kron_values(dot_last(pick_ref[...], wt_ref[...]), cols_ref[...])
-    dmat[...] = kron_values(jnp.dot(four_ref[...], dec_ref[...], preferred_element_type=F32), dcols_ref[...])
+    dmat[...] = kron_values(jnp.dot(four_ref[...], dec_ref[...], preferred_element_type=F32), cols_ref[...])
     for c in [*load_tabs, load_weights, load_inv, load_state]:
         c.wait()
 
     @pl.loop(0, ITERS)
     def _(it):
-        for h in range(2):
-            for k in range(early):
+        for e in range(2):
+            for h in range(2):
+                a = own[h][0]
+                for k in range(pieces):
+                    for d in range(1, 4):
+                        one(h, d, k, e).wait()
+
+                @pl.loop(2 * e, 2 * e + 2)
+                def _(n):
+                    cols = pl.ds(pl.multiple_of(n * 256, 256), 256)
+                    x = r1[h, :, :, cols].reshape(4 * ROWS, 256)
+                    pt = lax.dot_general(x, tabs[h], (((0,), (0,)), ((), ())), preferred_element_type=F32)
+                    pt = pt.reshape(2, 2, 2, 4, 8, 256)
+                    for pair in range(2):
+                        for h2 in range(2):
+                            q0, q1 = pt[pair, h2, 0], pt[pair, h2, 1]
+                            re = q0[..., :M] + q1[..., M:]
+                            im = q1[..., :M] - q0[..., M:]
+                            both = jnp.concatenate([re, im], 1)
+                            c = 2 * (2 * n + pair) + lax.rem(h2 + a, 2)
+                            part[h, :, c] = both
+                            s2[h, :, c] = both.astype(BF)
+
                 for d in range(1, 4):
-                    one(h, d, k).wait()
-
-            @pl.loop(0, 4)
-            def _(n):
-                cols = pl.ds(pl.multiple_of(n * 256, 256), 256)
-                x = r1[h, :, 0:64, cols].reshape(256, 256)
-                table = tabs[h].reshape(4, ROWS, 2 * M)[:, 0:64].reshape(256, 2 * M)
-                acc[h, n] = lax.dot_general(x, table, (((0,), (0,)), ((), ())), preferred_element_type=F32)
-
-        for h in range(2):
-            a, b = own[h]
-            for k in range(early, pieces):
-                for d in range(1, 4):
-                    one(h, d, k).wait()
-
-            @pl.loop(0, 4)
-            def _(n):
-                cols = pl.ds(pl.multiple_of(n * 256, 256), 256)
-                x = r1[h, :, 64:96, cols].reshape(128, 256)
-                table = tabs[h].reshape(4, ROWS, 2 * M)[:, 64:96].reshape(128, 2 * M)
-                pt = acc[h, n] + lax.dot_general(x, table, (((0,), (0,)), ((), ())), preferred_element_type=F32)
-                pt = pt.reshape(2, 2, 2, 4, 8, 256)
-                for pair in range(2):
-                    for h2 in range(2):
-                        q0, q1 = pt[pair, h2, 0], pt[pair, h2, 1]
-                        re = q0[..., :M] + q1[..., M:]
-                        im = q1[..., :M] - q0[..., M:]
-                        both = jnp.concatenate([re, im], 1)
-                        c = 2 * (2 * n + pair) + lax.rem(h2 + a, 2)
-                        part[h, :, c] = both
-                        s2[h, :, c] = both.astype(BF)
-
-            for d in range(1, 4):
-                two(h, d).start()
+                    two(h, d, e).start()
 
         prepare(0, SPLIT)
-        for h in range(2):
+        for e, h in ((0, 0), (0, 1), (1, 0), (1, 1)):
             b = own[h][1]
             for d in range(1, 4):
-                two(h, d).wait()
-
-            @pl.loop(0, 16)
+                two(h, d, e).wait()
+
+            @pl.loop(8 * e, 8 * e + 8)
             def _(c):
                 total = part[h, b, c]
                 for d in range(3):
@@ -424,91 +417,87 @@
                         return ar + (sr * wr - si * wi), ai + (sr * wi + si * wr)
 
                     re_at, im_at = pl.ds(j, 16, stride=16), pl.ds(8 + j, 16, stride=16)
-                    if h == 0:
+                    if e == 0 and h == 0:
                         begin = (jnp.zeros((16, M), F32), jnp.zeros((16, M), F32))
                     else:
                         begin = (mx[oh, re_at, :], mx[oh, im_at, :])
-                    ar, ai = lax.fori_loop(16 * h, 16 * h + 16, add, begin, unroll=8)
+                    ar, ai = lax.fori_loop(16 * h + 8 * e, 16 * h + 8 * e + 8, add, begin, unroll=8)
                     mx[oh, re_at, :] = ar
                     mx[oh, im_at, :] = ai
-                if h == 1:
+                if e == 1 and h == 1:
                     r3[oh, own[oh][1]] = mx[oh].reshape(16, 16, M).astype(BF)
-                    for d in range(1, 4):
-                        three(oh, d).start()
+                    for late in range(2):
+                        for d in range(1, 4):
+                            three(oh, d, late).start()
 
         prepare(SPLIT, 6)
 
-        def back_chunk(h, k):
+        def back_chunk(h, k, e):
             rows = rows_of(k)
             a = own[h][0]
             left = jnp.concatenate([tabs[h, pl.ds(pl.multiple_of(ROWS * p + k * YC, YC), YC)] for p in range(4)], 0)
-            for n in range(4):
+            for n in range(2 * e, 2 * e + 2):
                 lanes = slice(256 * n, 256 * n + 256)
                 out = lax.dot_general(left, m2[h, lanes], (((1,), (1,)), ((), ())), preferred_element_type=F32)
                 s4[h, :, rows, lanes] = out.reshape(4, YC, 256).astype(BF)
             for d in range(1, 4):
-                four(h, d, k).start()
-            back[h, a, rows] = s4[h, a, rows]
-
-        for h in range(2):
-            a = own[h][0]
-            for d in range(1, 4):
-                three(h, d).wait()
-
-            @pl.loop(0, 8)
-            def _(n):
-                rows = []
-                for h2 in range(2):
-                    c = 2 * n + lax.rem(h2 + a, 2)
-                    block = r3[h, :, c].astype(F32).reshape(4, 2, 8, M)
-                    re = block[:, 0].reshape(32, M)
-                    im = block[:, 1].reshape(32, M)
-                    rows.append(jnp.concatenate([re, -im], 1))
-                    rows.append(jnp.concatenate([im, re], 1))
-                m2[h, pl.ds(pl.multiple_of(n * 128, 128), 128)] = jnp.concatenate(rows, 0).astype(BF)
-
-            back_chunk(h, 0)
-
-        @pl.loop(1, chunks)
+                four(h, d, k, e).start()
+            back[h, a, rows, lanes_of(e)] = s4[h, a, rows, lanes_of(e)]
+
+        for e in range(2):
+            for h in range(2):
+                a = own[h][0]
+                for d in range(1, 4):
+                    three(h, d, e).wait()
+
+                @pl.loop(4 * e, 4 * e + 4)
+                def _(n):
+                    rows = []
+                    for h2 in range(2):
+                        c = 2 * n + lax.rem(h2 + a, 2)
+                        block = r3[h, :, c].astype(F32).reshape(4, 2, 8, M)
+                        re = block[:, 0].reshape(32, M)
+                        im = block[:, 1].reshape(32, M)
+                        rows.append(jnp.concatenate([re, -im], 1))
+                        rows.append(jnp.concatenate([im, re], 1))
+                    m2[h, pl.ds(pl.multiple_of(n * 128, 128), 128)] = jnp.concatenate(rows, 0).astype(BF)
+
+                back_chunk(h, 0, e)
+
+            @pl.loop(1, chunks)
+            def _(k):
+                for h in range(2):
+                    back_chunk(h, k, e)
+
+        @pl.when(it < ITERS - 1)
+        def _():
+            for e in range(2):
+                @pl.loop(0, chunks)
+                def _(k):
+                    for h in range(2):
+                        for d in range(1, 4):
+                            four(h, d, k, e).wait()
+                    update(k, keep_state, e)
+                    forward(k, lambda c, rows: state[c, rows], e)
+
+    for e in range(2):
+        @pl.loop(0, chunks)
         def _(k):
             for h in range(2):
-                back_chunk(h, k)
-
-        @pl.when(it < ITERS - 1)
-        def _():
-            @pl.loop(0, chunks)
-            def _(k):
-                for h in range(2):
-                    for d in range(1, 4):
-                        four(h, d, k).wait()
-
-                @pl.loop(0, YC // LC)
-                def _(t):
-                    update(k * (YC // LC) + t, keep_state)
-                    forward(k * (YC // LC) + t, lambda c, rows: state[c, rows])
-
-    @pl.loop(0, chunks)
-    def _(k):
-        for h in range(2):
-            for d in range(1, 4):
-                four(h, d, k).wait()
-
-        @pl.loop(0, YC // LC)
-        def _(t):
-            piece = k * (YC // LC) + t
-            rows = few_of(piece)
-            update(piece, keep_final)
-            for s in range(LC // 16):
-                part_rows = pl.ds(pl.multiple_of(piece * LC + 16 * s, 16), 16)
-                lhs = hold[:, 16 * s:16 * s + 16, :].reshape(C * 16, NX)
-                f = jnp.dot(dmat[...], lhs, preferred_element_type=F32)
-                fields[:, part_rows, :] = f.reshape(4, 16, NX)
+                for d in range(1, 4):
+                    four(h, d, k, e).wait()
+            update(k, keep_final, e)
+            if e == 1:
+                for s in range(YC // 16):
+                    rows = pl.ds(pl.multiple_of(k * YC + 16 * s, 16), 16)
+                    f = jnp.dot(dmat[...], state[:, rows, :].reshape(C * 16, NX), preferred_element_type=F32)
+                    fields[:, rows, :] = f.reshape(4, 16, NX)
 
     tail_body(fields, turning_ref, depth_ref, out_ref, own_heat, other_heat, chip, lower, total, share, up_out, up_in,
               geo, edge_out, edge_in, ts, tr)
 
 
-def steps(forcing, weights, ytab, fwd, inv, pick, wt, cols, four, dec, dcols, turning, bias, depth):
+def steps(forcing, weights, ytab, fwd, inv, pick, wt, cols, four, dec, turning, bias, depth):
     near_shape = (2, 4, ROWS, NX)
     chunks = ROWS // YC
     flat = (ROWS, NX)
@@ -517,7 +506,7 @@
     dma = pltpu.SemaphoreType.DMA
     return pl.pallas_call(
         steps_body, name="steps",
-        in_specs=[any_space] * 5 + [vmem] * 7 + [SMEM] * 2,
+        in_specs=[any_space] * 5 + [vmem] * 6 + [SMEM] * 2,
         out_specs=[vmem, vmem],
         out_shape=[pltpu.VMEM((C, ROWS, NX), F32), pltpu.VMEM((3, ROWS, NX), F32)],
         scratch_shapes=[
@@ -535,23 +524,22 @@
             pltpu.VMEM((2, 3, 16, 16, M), BF),
             pltpu.VMEM((C, 16, M), F32),
             pltpu.VMEM((2, 16 * 16, M), F32),
-            pltpu.VMEM((2, 4, 256, 256), F32),
             pltpu.VMEM((2, 4, 16, 16, M), BF),
             pltpu.VMEM((2, NX, 2 * M), BF),
             pltpu.VMEM(near_shape, BF),
             pltpu.VMEM(near_shape, BF),
-            pltpu.VMEM((64, C * 16), BF), pltpu.VMEM((C, LC, NX), BF),
+            pltpu.VMEM((64, C * 16), BF),
             pltpu.VMEM((4, ROWS, NX), F32),
             pltpu.VMEM(flat, BF), pltpu.VMEM(flat, BF), pltpu.VMEM((48, NX), BF), pltpu.VMEM((3, 48, NX), BF),
             pltpu.VMEM(flat, F32), pltpu.VMEM((48, NX), F32), pltpu.VMEM(flat, BF), pltpu.VMEM(flat, BF),
             pltpu.VMEM(flat, F32), pltpu.VMEM((2, 8, NX), F32), pltpu.VMEM((4, 8, NX), F32), dma((10,)), dma((10,)),
             dma((9,)),
-            dma((2, 3, ROWS // LC)), dma((2, 3, ROWS // LC)),
-            dma((2, 3)), dma((2, 3)), dma((2, 3)), dma((2, 3)),
-            dma((2, 3, chunks)), dma((2, 3, chunks)),
+            dma((2, 2, 3, chunks)), dma((2, 2, 3, chunks)),
+            dma((2, 2, 3)), dma((2, 2, 3)), dma((2, 2, 3)), dma((2, 2, 3)),
+            dma((2, 2, 3, chunks)), dma((2, 2, 3, chunks)),
         ],
         compiler_params=pltpu.CompilerParams(collective_id=1, has_side_effects=True, vmem_limit_bytes=LIMIT),
-    )(forcing, weights, ytab, fwd, inv, pick, wt, cols, four, dec, dcols, turning, bias, depth)
+    )(forcing, weights, ytab, fwd, inv, pick, wt, cols, four, dec, turning, bias, depth)
 
 
 def finish_body(final_ref, residual_ref, final_out, residual_out, sem):
@@ -580,15 +568,15 @@
     pick[np.arange(C), order] = 1.0
     spread = np.repeat(np.eye(C, dtype=np.float32), 16, 1)
     four = np.repeat(np.eye(4, dtype=np.float32), 16, 0)
-    return [v.astype(BF) for v in (np.repeat(pick, 16, 0), spread, four, pick.T @ spread)]
+    return [v.astype(BF) for v in (np.repeat(pick, 16, 0), spread, four)]
 
 
 def on_device(forcing, spectral_weight, point_weight, point_bias, decoder, coriolis, layer_depth):
     source = forcing[0]
     fwd, inv = (jnp.asarray(v) for v in x_tables())
     ytab = jnp.asarray(y_tables())
-    pick, cols, four, dec_cols = [jnp.asarray(v) for v in kron_parts()]
-    final, residual = steps(source, spectral_weight, ytab, fwd, inv, pick, point_weight, cols, four, decoder, dec_cols,
+    pick, cols, four = [jnp.asarray(v) for v in kron_parts()]
+    final, residual = steps(source, spectral_weight, ytab, fwd, inv, pick, point_weight, cols, four, decoder,
                             coriolis[None], point_bias, layer_depth)
     final, residual = finish(final, residual)
     return final[None], residual[:, None]

time: 130 us -> 119 us (0.915)
  Pallas kernels: 128 us -> 119 us
    pallas_call x1, Pallas kernels: 123 us -> 114 us  [steps(): pl.pallas_call(steps_body, name='steps', in_specs=[any_space] * 5 + [vmem...]
where the time goes in v6:
time: 119 us
  Pallas kernels  119 us (100%)
    pallas_call x1, Pallas kernels, steps(): pl.pallas_call(steps_body, name='steps', in_specs=[any_space] * 5 + [vmem...  114 us
    pallas_call x1, Pallas kernels, finish(): pl.pallas_call(finish_body, name='finish', in_specs=[pl.BlockSpec(memory_...  5.01 us

profile of v6, /device:TPU:2, one launch (start us, length us, event | category | flops | bytes accessed | tf_op | source)
XLA Modules:
  0.0 119.2 jit_solution(4998661718733010375)
XLA Ops:
  0.6 113.5 %steps.1 = (f32[32,96,1024]{2,1,0:T(8,128)S(1)}, f32[3,96,1024]{2,1,0:T(8,128)S(1)}) custom-call(bf16[32,96,1024]{2,1,0:T(8,128)(2,1)} %bitcast.6, bf16[2,8,32,32,128]{4,3,2,1,0:T(8,128)(2,1)} %weight_ref.1, bf16[2,4,384,256]{3,2,1,0:T(8,128)(2,1)} %constant.14.clone.ytab_ref, bf16[4,1024,256]{2,1,0:T(8,128)(2,1)} %constant.12.clone.fwd_hbm, ...), custom_call_target="tpu_custom_call" | custom-call | tf_op jit(solution)/shard_map/steps/pallas_call | solution.py:507
  114.2 5.0 %finish.1 = (f32[32,96,1024]{2,1,0:T(8,128)}, f32[3,96,1024]{2,1,0:T(8,128)}) custom-call(f32[32,96,1024]{2,1,0:T(8,128)S(1)} %get-tuple-element.6.final_ref, f32[3,96,1024]{2,1,0:T(8,128)S(1)} %get-tuple-element.7.residual_ref), custom_call_target="tpu_custom_call" | custom-call | tf_op jit(solution)/shard_map/finish/pallas_call | solution.py:556

commit v7 on v6

--- a/solution.py
+++ b/solution.py
@@ -18,8 +18,8 @@
 MESH = pl.DeviceIdType.MESH
 BF = jnp.bfloat16
 F32 = jnp.float32
-YC = 32
-LC = 32
+YC = 48
+LC = 48
 SPLIT = 3
 TILE = 256
 

time: 119 us -> 119 us (level)
  no operation moved by 1% of the time
where the time goes in v7:
time: 119 us
  Pallas kernels  118 us (99%)
    pallas_call x1, Pallas kernels, steps(): pl.pallas_call(steps_body, name='steps', in_specs=[any_space] * 5 + [vmem...  113 us
    pallas_call x1, Pallas kernels, finish(): pl.pallas_call(finish_body, name='finish', in_specs=[pl.BlockSpec(memory_...  5.01 us

profile of v7, /device:TPU:2, one launch (start us, length us, event | category | flops | bytes accessed | tf_op | source)
XLA Modules:
  0.0 118.6 jit_solution(3036485119364653091)
XLA Ops:
  0.6 113.0 %steps.1 = (f32[32,96,1024]{2,1,0:T(8,128)S(1)}, f32[3,96,1024]{2,1,0:T(8,128)S(1)}) custom-call(bf16[32,96,1024]{2,1,0:T(8,128)(2,1)} %bitcast.6, bf16[2,8,32,32,128]{4,3,2,1,0:T(8,128)(2,1)} %weight_ref.1, bf16[2,4,384,256]{3,2,1,0:T(8,128)(2,1)} %constant.14.clone.ytab_ref, bf16[4,1024,256]{2,1,0:T(8,128)(2,1)} %constant.12.clone.fwd_hbm, ...), custom_call_target="tpu_custom_call" | custom-call | tf_op jit(solution)/shard_map/steps/pallas_call | solution.py:507
  113.6 5.0 %finish.1 = (f32[32,96,1024]{2,1,0:T(8,128)}, f32[3,96,1024]{2,1,0:T(8,128)}) custom-call(f32[32,96,1024]{2,1,0:T(8,128)S(1)} %get-tuple-element.6.final_ref, f32[3,96,1024]{2,1,0:T(8,128)S(1)} %get-tuple-element.7.residual_ref), custom_call_target="tpu_custom_call" | custom-call | tf_op jit(solution)/shard_map/finish/pallas_call | solution.py:556
